TPU v7x, 128 devices: a whole 4x4x4 slice. The times are simulated.
128 devices in a mesh: seq: 8 (over x, core), tp: 16 (over z, y).
Axes of the slice: x: 4, y: 4, z: 4, core: 2. Of those that a mesh axis runs over, the one named last changes fastest.
Arguments:
- tokens: bfloat16 [2048, 4096], P('seq', 'tp'), may hold values from -12 to 12
- norm_gain: float32 [2, 4096], replicated, may hold values from 0.5 to 1.5
- w_in: bfloat16 [2, 4096, 2, 8192], P(None, None, None, 'tp'), may hold values from -0.09375 to 0.09375
- w_low: bfloat16 [2, 4096, 288], P(None, 'tp'), may hold values from -0.09375 to 0.09375
- w_dt: bfloat16 [2, 256, 8192], P(None, None, 'tp'), may hold values from -0.75 to 0.75
- a_rate: float32 [2, 16, 8192], P(None, None, 'tp'), may hold values from 0.00024414062 to 0.2
- dt_bias: float32 [2, 8192], P(None, 'tp'), may hold values from -5 to -1
- skip_gain: float32 [2, 8192], P(None, 'tp'), may hold values from 0.5 to 1.5
- threshold: float32 [2, 8192], P(None, 'tp'), may hold values from 0.1 to 0.8
- w_out: bfloat16 [2, 8192, 4096], P(None, 'tp'), may hold values from -0.09375 to 0.09375
Outputs:
- hidden: bfloat16 [2048, 4096], P('seq', 'tp')
All inputs are finite; a program needn't handle non-finite values.
Results may differ from a plain program's by a relative error of at most 0.019.
Values may be sent and summed in bfloat16 or wider, within the bound.
A program may use at most 128 MiB of HBM per device.

v0:
```python
import functools
import math

import jax
import jax.numpy as jnp
from jax import lax
from jax.experimental import pallas as pl
from jax.experimental.pallas import tpu as pltpu
from jax.sharding import PartitionSpec as P

MESH = pl.DeviceIdType.MESH
F32 = jnp.float32
BF16 = jnp.bfloat16
SUB = 8
LANE = 128
SIDE = 4
LOG2E = math.log2(math.e)
OFFS = (0, -1, 1, 2)


def kernel_body(
    dims,
    tok_ref,
    gain_ref,
    w_in_hbm,
    w_low_hbm,
    w_dt_hbm,
    a_ref,
    bias_ref,
    skip_ref,
    thresh_ref,
    w_out_hbm,
    out_ref,
    w_in_v,
    w_low_v,
    w_dt_v,
    w_out_v,
    hid,
    agbuf,
    selp,
    arrecv,
    arres,
    expand_b,
    expand_c,
    bx,
    cx,
    step,
    cum,
    proj,
    yv,
    pin,
    ein,
    hdev,
    esend_f,
    esend,
    erecv,
    tsend,
    trecv,
    gated,
    pbuf,
    x1,
    x2,
    s2,
    x3,
    x4,
    wsem,
    ag_s,
    ag_r,
    ar1_s,
    ar1_r,
    ar2_s,
    ar2_r,
    t_s,
    t_r,
    e_s,
    e_r,
    rs_s,
    rs_r,
):
    layers, n_seq, toks, feat, chans, states, rank = dims
    n_tp = SIDE * SIDE
    half = toks // 2
    quart = toks // 4
    steps = toks // SUB
    arow = toks // n_tp
    ncb = chans // LANE
    seqi = lax.axis_index("seq")
    tpi = lax.axis_index("tp")
    zc = tpi // SIDE
    yc = lax.rem(tpi, SIDE)

    def wrap(v):
        return lax.rem(v + 2 * SIDE, SIDE)

    pos = ((yc, zc), (zc, yc))

    def blk(h, c1, c2):
        return c2 * SIDE + c1 if h == 0 else c1 * SIDE + c2

    def nb(h, axis, d):
        p1, p2 = pos[h]
        if axis == 1:
            return {"tp": blk(h, wrap(p1 + d), p2)}
        return {"tp": blk(h, p1, wrap(p2 + d))}

    def rcopy(src, dst, ssem, rsem, dev):
        return pltpu.make_async_remote_copy(
            src_ref=src, dst_ref=dst, send_sem=ssem, recv_sem=rsem,
            device_id=dev, device_id_type=MESH,
        )

    def wcopies(l):
        return (
            pltpu.make_async_copy(w_low_hbm.at[l], w_low_v.at[l, : rank + 2 * states], wsem.at[l, 0]),
            pltpu.make_async_copy(w_dt_hbm.at[l], w_dt_v.at[l], wsem.at[l, 1]),
            pltpu.make_async_copy(w_in_hbm.at[l], w_in_v.at[l], wsem.at[l, 2]),
            pltpu.make_async_copy(w_out_hbm.at[l], w_out_v.at[l], wsem.at[l, 3]),
        )

    for l in range(layers):
        for c in wcopies(l):
            c.start()

    barrier = pltpu.get_barrier_semaphore()
    for d in range(1, n_tp):
        pl.semaphore_signal(barrier, inc=1, device_id={"tp": lax.rem(tpi + d, n_tp)}, device_id_type=MESH)
    for d in range(1, n_seq):
        pl.semaphore_signal(barrier, inc=1, device_id={"seq": lax.rem(seqi + d, n_seq)}, device_id_type=MESH)
    pl.semaphore_wait(barrier, n_tp + n_seq - 2)

    ri = lax.broadcasted_iota(jnp.int32, (toks, toks), 0)
    ci = lax.broadcasted_iota(jnp.int32, (toks, toks), 1)
    perm = jnp.where(ci == lax.rem(ri, SUB) * steps + ri // SUB, 1.0, 0.0).astype(BF16)
    hid[...] = jnp.dot(perm, tok_ref[...], preferred_element_type=F32).astype(BF16)

    ei = lax.broadcasted_iota(jnp.int32, (LANE, states * LANE), 0)
    ej = lax.broadcasted_iota(jnp.int32, (LANE, states * LANE), 1) // LANE
    expand_b[...] = jnp.where(ei == ej, 1.0, 0.0).astype(BF16)
    expand_c[...] = jnp.where(ei == ej + states, 1.0, 0.0).astype(BF16)
    sel_w = rank + LANE
    pad_from = rank + 2 * states
    for l in range(layers):
        w_low_v[l, pad_from:, :] = jnp.zeros((sel_w - pad_from, feat), BF16)

    def ag_info(h, k):
        p1, p2 = pos[h]
        r0 = h * half
        full = pl.ds(r0, half)
        lo = pl.ds(r0, quart)
        hi = pl.ds(r0 + quart, quart)
        if k < 4:
            m = k
            ax = 1

            def at(d):
                return blk(h, wrap(p1 + d), p2)
        else:
            m = (k - 4) % 4
            o = OFFS[(k - 4) // 4]
            ax = 2

            def at(d):
                return blk(h, wrap(p1 + o), wrap(p2 + d))

        src_d, dst_d, rows, to = (
            (0, -1, full, 1),
            (0, 1, full, -1),
            (-1, -2, lo, 1),
            (1, 2, hi, -1),
        )[m]
        return at(src_d), at(dst_d), rows, nb(h, ax, to)

    def ag_send(h, k):
        src, _, rows, dev = ag_info(h, k)
        ref = agbuf.at[src, rows]
        return rcopy(ref, ref, ag_s.at[h, k], ag_r.at[h, k], dev)

    def ag_start(*ks):
        for k in ks:
            for h in range(2):
                ag_send(h, k).start()

    def ag_wait(*ks):
        for k in ks:
            for h in range(2):
                _, dst, rows, dev = ag_info(h, k)
                ref = agbuf.at[dst, rows]
                rcopy(ref, ref, ag_s.at[h, k], ag_r.at[h, k], dev).wait_recv()

    def layer(l, unused):
        low_c, dt_c, in_c, out_c = wcopies(l)
        own = hid[...].astype(F32)
        gain_row = gain_ref[pl.ds(l, 1), pl.ds(pl.multiple_of(tpi * feat, feat), feat)]
        agbuf[tpi] = (own * gain_row).astype(BF16)
        sq = jnp.sum(own * own, axis=1, keepdims=True)
        ag_start(0, 1, 4, 5)

        low_c.wait()
        selv = lax.dot_general(
            agbuf[tpi], w_low_v[l], (((1,), (1,)), ((), ())), preferred_element_type=F32
        )
        sq_hi = sq.astype(BF16).astype(F32)
        lane = lax.broadcasted_iota(jnp.int32, (toks, sel_w), 1)
        selv = jnp.where(lane == pad_from, sq_hi, selv)
        selv = jnp.where(lane == pad_from + 1, sq - sq_hi, selv)
        selp[...] = selv.astype(BF16)
        arrecv[tpi] = selp[pl.ds(pl.multiple_of(tpi * arow, arow), arow), :]

        def ar1(d, sending):
            to = lax.rem(tpi + d, n_tp)
            fr = lax.rem(tpi + n_tp - d, n_tp)
            rows = pl.ds(pl.multiple_of(to * arow, arow), arow)
            dst = arrecv.at[tpi] if sending else arrecv.at[fr]
            return rcopy(selp.at[rows], dst, ar1_s.at[d], ar1_r.at[d], {"tp": to})

        for d in range(1, n_tp):
            ar1(d, True).start()

        ag_wait(0, 1)
        ag_start(2, 3, 8, 9, 12, 13)

        for d in range(1, n_tp):
            ar1(d, False).wait_recv()
        tot = jnp.zeros((arow, sel_w), F32)
        for i in range(n_tp):
            tot = tot + arrecv[i].astype(F32)
        lane = lax.broadcasted_iota(jnp.int32, (arow, sel_w), 1)
        is_sq = (lane == pad_from) | (lane == pad_from + 1)
        ssum = jnp.sum(jnp.where(is_sq, tot, 0.0), axis=1, keepdims=True)
        factor = lax.rsqrt(ssum / (n_tp * feat) + 1e-05)
        f_hi = factor.astype(BF16).astype(F32)
        tot = jnp.where(lane == pad_from, f_hi, jnp.where(lane == pad_from + 1, factor - f_hi, tot * factor))
        mine = pl.ds(pl.multiple_of(tpi * arow, arow), arow)
        arres[mine, :] = tot.astype(BF16)

        def ar2(d, sending):
            to = lax.rem(tpi + d, n_tp)
            fr = lax.rem(tpi + n_tp - d, n_tp)
            base = tpi if sending else fr
            rows = pl.ds(pl.multiple_of(base * arow, arow), arow)
            return rcopy(arres.at[rows], arres.at[rows], ar2_s.at[d], ar2_r.at[d], {"tp": to})

        for d in range(1, n_tp):
            ar2(d, True).start()

        ag_wait(4, 5)
        ag_start(6, 7)
        ag_wait(2, 3)
        ag_start(16, 17)

        for d in range(1, n_tp):
            ar2(d, False).wait_recv()
        tail = arres[:, rank:]
        tl = lax.broadcasted_iota(jnp.int32, (toks, LANE), 1)
        in_f = (tl == 2 * states) | (tl == 2 * states + 1)
        fac = jnp.sum(jnp.where(in_f, tail.astype(F32), 0.0), axis=1, keepdims=True)
        dt_c.wait()
        pre = jnp.dot(arres[:, :rank], w_dt_v[l], preferred_element_type=F32) + bias_ref[pl.ds(l, 1), :]
        step[...] = jnp.maximum(pre, 0.0) + jnp.log1p(jnp.exp(-jnp.abs(pre)))
        bx[...] = jnp.dot(tail, expand_b[...], preferred_element_type=F32)
        cx[...] = jnp.dot(tail, expand_c[...], preferred_element_type=F32)

        def accum(t, run):
            rows = pl.ds(pl.multiple_of(t * SUB, SUB), SUB)
            run = run + step[rows, :]
            cum[rows, :] = run
            return run

        ctot = lax.fori_loop(0, steps, accum, jnp.zeros((SUB, chans), F32))
        tsend[l] = jnp.broadcast_to(jnp.sum(ctot, axis=0, keepdims=True), (SUB, chans))

        def seq_copy(src, dst, ss, rs, q, sending):
            slot = seqi if sending else q
            return rcopy(src, dst.at[l, slot], ss.at[l, q], rs.at[l, slot], {"seq": q})

        for q in range(1, n_seq):
            @pl.when(q > seqi)
            def _():
                seq_copy(tsend.at[l], trecv, t_s, t_r, q, True).start()

        ag_wait(8, 9)
        ag_start(10, 11)
        ag_wait(12, 13)
        ag_start(14, 15)

        in_c.wait()

        def mm(first, pairs):
            for i, (dz, dy) in enumerate(pairs):
                b = wrap(zc + dz) * SIDE + wrap(yc + dy)
                rows = pl.ds(pl.multiple_of(b * feat, feat), feat)
                val = jnp.dot(agbuf[b], w_in_v[l, rows, :], preferred_element_type=F32)
                if first and i == 0:
                    proj[...] = val
                else:
                    proj[...] += val

        mm(True, ((0, 0), (0, 1), (0, -1), (1, 0), (-1, 0), (1, 1), (1, -1), (-1, 1), (-1, -1)))
        ag_wait(16, 17)
        ag_start(18, 19)
        ag_wait(6, 7, 10, 11, 14, 15, 18, 19)
        mm(False, ((2, 0), (2, 1), (2, 2), (2, 3), (0, 2), (1, 2), (3, 2)))
        proj[...] = proj[...] * fac
        for k in range(20):
            for h in range(2):
                ag_send(h, k).wait_send()
        for d in range(1, n_tp):
            ar1(d, True).wait_send()
            ar2(d, True).wait_send()

        skip_row = skip_ref[pl.ds(l, 1), :]
        th_row = thresh_ref[pl.ds(l, 1), :]
        for cb in range(ncb):
            cs = pl.ds(cb * LANE, LANE)
            na = [
                jnp.broadcast_to(a_ref[l, s : s + 1, cs] * (-LOG2E), (SUB, LANE)) for s in range(states)
            ]
            skip = skip_row[:, cb * LANE : (cb + 1) * LANE]

            def scan_step(t, hs):
                rows = pl.ds(pl.multiple_of(t * SUB, SUB), SUB)
                st = step[rows, cs]
                cur = proj[rows, cs]
                dr = st * cur
                acc = skip * cur
                new = []
                for s in range(states):
                    ls = pl.ds(s * LANE, LANE)
                    hn = jnp.exp2(st * na[s]) * hs[s] + bx[rows, ls] * dr
                    acc = acc + cx[rows, ls] * hn
                    new.append(hn)
                yv[rows, cs] = acc
                return tuple(new)

            hs = lax.fori_loop(
                0, steps, scan_step, tuple(jnp.zeros((SUB, LANE), F32) for _ in range(states))
            )
            sub = lax.broadcasted_iota(jnp.int32, (SUB, LANE), 0)
            ct = cum[pl.ds((steps - 1) * SUB, SUB), cs]
            for s in range(states):
                e = hs[s]
                p = jnp.exp2(ct * na[s])
                for d in (1, 2, 4):
                    ok = sub >= d
                    e = e + jnp.where(ok, p * pltpu.roll(e, d, 0), 0.0)
                    p = p * jnp.where(ok, pltpu.roll(p, d, 0), 1.0)
                esend_f[s : s + 1, cs] = e[SUB - 1 : SUB, :]
                ein[s, :, cs] = jnp.where(sub >= 1, pltpu.roll(e, 1, 0), 0.0)
                pin[s, :, cs] = jnp.where(sub >= 1, pltpu.roll(p, 1, 0), 1.0)

        esend[l] = esend_f[...].astype(BF16)
        for q in range(1, n_seq):
            @pl.when(q > seqi)
            def _():
                seq_copy(esend.at[l], erecv, e_s, e_r, q, True).start()

        hdev[...] = jnp.zeros_like(hdev)
        for q in range(n_seq - 1):
            @pl.when(q < seqi)
            def _():
                seq_copy(tsend.at[l], trecv, t_s, t_r, q, False).wait_recv()
                seq_copy(esend.at[l], erecv, e_s, e_r, q, False).wait_recv()
                dec = jnp.exp2(a_ref[l] * (-LOG2E) * trecv[l, q, 0:1, :])
                hdev[...] = dec * hdev[...] + erecv[l, q].astype(F32)

        for cb in range(ncb):
            cs = pl.ds(cb * LANE, LANE)
            na = [
                jnp.broadcast_to(a_ref[l, s : s + 1, cs] * (-LOG2E), (SUB, LANE)) for s in range(states)
            ]
            hin = [ein[s, :, cs] + pin[s, :, cs] * hdev[s : s + 1, cs] for s in range(states)]
            th = th_row[:, cb * LANE : (cb + 1) * LANE]

            def fold(t, unused):
                rows = pl.ds(pl.multiple_of(t * SUB, SUB), SUB)
                ct = cum[rows, cs]
                acc = yv[rows, cs]
                for s in range(states):
                    ls = pl.ds(s * LANE, LANE)
                    acc = acc + cx[rows, ls] * (jnp.exp2(ct * na[s]) * hin[s])
                yv[rows, cs] = acc
                return unused

            lax.fori_loop(0, steps, fold, 0)

            mixed = yv[:, cs]
            fct = lax.rsqrt(jnp.mean(mixed * mixed, axis=1, keepdims=True) + 1e-05)
            normal = mixed * fct
            shrunk = jnp.maximum(normal - th, 0.0) - jnp.maximum(-normal - th, 0.0)
            gate = proj[:, pl.ds(chans + cb * LANE, LANE)]
            gated[:, cs] = (shrunk * (gate / (1.0 + jnp.exp(-gate)))).astype(BF16)

        for q in range(1, n_seq):
            @pl.when(q > seqi)
            def _():
                seq_copy(tsend.at[l], trecv, t_s, t_r, q, True).wait_send()
                seq_copy(esend.at[l], erecv, e_s, e_r, q, True).wait_send()

        out_c.wait()
        lo = pl.ds(0, quart)
        hi = pl.ds(quart, quart)

        def rpos(h):
            p2, p1 = pos[h]
            return p1, p2

        def rnb(h, axis, d):
            return nb(h, 3 - axis, d)

        def omm(h, c1):
            lhs = gated[h * half : (h + 1) * half, :]
            for c2 in range(SIDE):
                b = c1 * SIDE + c2 if h == 0 else c2 * SIDE + c1
                cols = pl.ds(pl.multiple_of(b * feat, feat), feat)
                pbuf[h, c1, c2] = jnp.dot(
                    lhs, w_out_v[l, :, cols], preferred_element_type=F32
                ).astype(BF16)

        def rs_copy(h, k):
            p1, p2 = rpos(h)
            src, dst, dev = (
                lambda: (pbuf.at[h, wrap(p1 + 2), :, lo], x1.at[h, 0], rnb(h, 1, 1)),
                lambda: (pbuf.at[h, wrap(p1 + 2), :, hi], x1.at[h, 1], rnb(h, 1, -1)),
                lambda: (pbuf.at[h, wrap(p1 + 1)], x2.at[h, 0], rnb(h, 1, 1)),
                lambda: (pbuf.at[h, wrap(p1 - 1)], x2.at[h, 1], rnb(h, 1, -1)),
                lambda: (s2.at[h, wrap(p2 + 2), lo], x3.at[h, 0], rnb(h, 2, 1)),
                lambda: (s2.at[h, wrap(p2 + 2), hi], x3.at[h, 1], rnb(h, 2, -1)),
                lambda: (s2.at[h, wrap(p2 + 1)], x4.at[h, 0], rnb(h, 2, 1)),
                lambda: (s2.at[h, wrap(p2 - 1)], x4.at[h, 1], rnb(h, 2, -1)),
            )[k]()
            return rcopy(src, dst, rs_s.at[h, k], rs_r.at[h, k], dev)

        for h in range(2):
            omm(h, wrap(rpos(h)[0] + 2))
            rs_copy(h, 0).start()
            rs_copy(h, 1).start()
        for h in range(2):
            omm(h, wrap(rpos(h)[0] + 1))
            omm(h, wrap(rpos(h)[0] - 1))
        for h in range(2):
            p1, _ = rpos(h)
            up = wrap(p1 + 1)
            dn = wrap(p1 - 1)
            rs_copy(h, 0).wait_recv()
            pbuf[h, up, :, lo] = (pbuf[h, up, :, lo].astype(F32) + x1[h, 0].astype(F32)).astype(BF16)
            rs_copy(h, 2).start()
            rs_copy(h, 1).wait_recv()
            pbuf[h, dn, :, hi] = (pbuf[h, dn, :, hi].astype(F32) + x1[h, 1].astype(F32)).astype(BF16)
            rs_copy(h, 3).start()
        for h in range(2):
            omm(h, rpos(h)[0])
        for h in range(2):
            p1, p2 = rpos(h)
            rs_copy(h, 2).wait_recv()
            rs_copy(h, 3).wait_recv()

            def sum3(c2):
                return pbuf[h, p1, c2].astype(F32) + x2[h, 0, c2].astype(F32) + x2[h, 1, c2].astype(F32)

            far = wrap(p2 + 2)
            s2[h, far] = sum3(far).astype(BF16)
            rs_copy(h, 4).start()
            rs_copy(h, 5).start()
            for d in (1, -1):
                c2 = wrap(p2 + d)
                s2[h, c2] = sum3(c2).astype(BF16)
        for h in range(2):
            p1, p2 = rpos(h)
            up = wrap(p2 + 1)
            dn = wrap(p2 - 1)
            rs_copy(h, 4).wait_recv()
            s2[h, up, lo] = (s2[h, up, lo].astype(F32) + x3[h, 0].astype(F32)).astype(BF16)
            rs_copy(h, 6).start()
            rs_copy(h, 5).wait_recv()
            s2[h, dn, hi] = (s2[h, dn, hi].astype(F32) + x3[h, 1].astype(F32)).astype(BF16)
            rs_copy(h, 7).start()
        for h in range(2):
            p1, p2 = rpos(h)
            rs_copy(h, 6).wait_recv()
            rs_copy(h, 7).wait_recv()
            total = pbuf[h, p1, p2].astype(F32) + x2[h, 0, p2].astype(F32) + x2[h, 1, p2].astype(F32)
            total = total + x4[h, 0].astype(F32) + x4[h, 1].astype(F32)
            rows = pl.ds(h * half, half)
            hid[rows, :] = (hid[rows, :].astype(F32) + total).astype(BF16)
        for h in range(2):
            for k in range(8):
                rs_copy(h, k).wait_send()
        return unused

    lax.fori_loop(0, layers, layer, 0)
    out_ref[...] = lax.dot_general(
        perm, hid[...], (((0,), (0,)), ((), ())), preferred_element_type=F32
    ).astype(BF16)


def per_device(n_seq, tokens, norm_gain, w_in, w_low, w_dt, a_rate, dt_bias, skip_gain, threshold, w_out):
    toks, feat = tokens.shape
    layers, model, _, chans = w_in.shape
    states = a_rate.shape[1]
    rank = w_dt.shape[1]
    n_tp = SIDE * SIDE
    half, quart = toks // 2, toks // 4
    sel_w = rank + LANE
    dims = (layers, n_seq, toks, feat, chans, states, rank)
    vm = pl.BlockSpec(memory_space=pltpu.VMEM)
    hb = pl.BlockSpec(memory_space=pl.ANY)
    dma = pltpu.SemaphoreType.DMA
    V = pltpu.VMEM
    return pl.pallas_call(
        functools.partial(kernel_body, dims),
        out_shape=jax.ShapeDtypeStruct((toks, feat), BF16),
        in_specs=[vm, vm, hb, hb, hb, vm, vm, vm, vm, hb],
        out_specs=vm,
        scratch_shapes=[
            V((layers, model, 2 * chans), BF16),
            V((layers, sel_w, feat), BF16),
            V((layers, rank, chans), BF16),
            V((layers, chans, model), BF16),
            V((toks, feat), BF16),
            V((n_tp, toks, feat), BF16),
            V((toks, sel_w), BF16),
            V((n_tp, toks // n_tp, sel_w), BF16),
            V((toks, sel_w), BF16),
            V((LANE, states * LANE), BF16),
            V((LANE, states * LANE), BF16),
            V((toks, states * LANE), F32),
            V((toks, states * LANE), F32),
            V((toks, chans), F32),
            V((toks, chans), F32),
            V((toks, 2 * chans), F32),
            V((toks, chans), F32),
            V((states, SUB, chans), F32),
            V((states, SUB, chans), F32),
            V((states, chans), F32),
            V((states, chans), F32),
            V((layers, states, chans), BF16),
            V((layers, n_seq, states, chans), BF16),
            V((layers, SUB, chans), F32),
            V((layers, n_seq, SUB, chans), F32),
            V((toks, chans), BF16),
            V((2, SIDE, SIDE, half, feat), BF16),
            V((2, 2, SIDE, quart, feat), BF16),
            V((2, 2, SIDE, half, feat), BF16),
            V((2, SIDE, half, feat), BF16),
            V((2, 2, quart, feat), BF16),
            V((2, 2, half, feat), BF16),
            dma((layers, 4)),
            dma((2, 20)),
            dma((2, 20)),
            dma((n_tp,)),
            dma((n_tp,)),
            dma((n_tp,)),
            dma((n_tp,)),
            dma((layers, n_seq)),
            dma((layers, n_seq)),
            dma((layers, n_seq)),
            dma((layers, n_seq)),
            dma((2, 8)),
            dma((2, 8)),
        ],
        compiler_params=pltpu.CompilerParams(
            collective_id=0, has_side_effects=True, vmem_limit_bytes=60 * 1024 * 1024
        ),
    )(
        tokens,
        norm_gain,
        w_in.reshape(layers, model, 2 * chans),
        jnp.swapaxes(w_low, 1, 2),
        w_dt,
        a_rate,
        dt_bias,
        skip_gain,
        threshold,
        w_out,
    )


def solution(mesh):
    in_specs = (
        P("seq", "tp"),
        P(),
        P(None, None, None, "tp"),
        P(None, "tp", None),
        P(None, None, "tp"),
        P(None, None, "tp"),
        P(None, "tp"),
        P(None, "tp"),
        P(None, "tp"),
        P(None, "tp", None),
    )
    return jax.shard_map(
        functools.partial(per_device, mesh.shape["seq"]),
        mesh=mesh,
        in_specs=in_specs,
        out_specs=P("seq", "tp"),
        check_vma=False,
    )
```

profile of v0, /device:TPU:6, one launch (start us, length us, event | category | flops | bytes accessed | tf_op | source)
XLA Modules:
  0.0 149.9 jit_solution(2548505104195614614)
XLA Ops:
  0.0 27.3 %reshape.3.w_in_hbm = bf16[2,4096,1024]{2,1,0:T(8,128)(2,1)} reshape(bf16[2,4096,2,512]{3,2,1,0:T(2,128)(2,1)} %param.12) | data formatting | bytes 33554432 | tf_op jit(solution)/shard_map/reshape | solution.py:567
  27.3 121.0 %shard_map.100 = bf16[256,256]{1,0:T(8,128)(2,1)} custom-call(bf16[256,256]{1,0:T(8,128)(2,1)} %tok_ref.1, f32[2,4096]{1,0:T(2,128)} %gain_ref.1, bf16[2,4096,1024]{2,1,0:T(8,128)(2,1)} %reshape.3.w_in_hbm, bf16[2,288,256]{2,1,0:T(8,128)(2,1)} %bitcast.1, bf16[2,256,512]{2,1,0:T(8,128)(2,1)} %w_dt_hbm.1, f32[2,16,512]{2,1,0:T(8,128)} %a_ref.1, ...), custom_call_target="tpu_custom_call" | custom-call | tf_op jit(solution)/shard_map/pallas_call | solution.py:509
  148.3 1.6 %copy.12 = bf16[256,256]{1,0:T(8,128)(2,1)} copy(bf16[256,256]{1,0:T(8,128)(2,1)} %shard_map.100) | data formatting | bytes 262144
where the time goes:
time: 151 us; the launch traced here: 150 us
  Pallas kernels  121 us (80%)
  local copies, waits for them, and re-layouts  28.9 us (19%)
    pallas_call x1, Pallas kernels, per_device(): pl.pallas_call(functools.partial(kernel_body, dims), out_shape=jax.ShapeD...  121 us
    reshape x1, local copies, waits for them, and re-layouts, per_device(): w_in.reshape(layers, model, 2 * chans)  27.3 us

commit v1 on v0

v1 whole, which is shorter than its diff:
```python
import functools
import math

import jax
import jax.numpy as jnp
from jax import lax
from jax.experimental import pallas as pl
from jax.experimental.pallas import tpu as pltpu
from jax.sharding import PartitionSpec as P

MESH = pl.DeviceIdType.MESH
F32 = jnp.float32
BF16 = jnp.bfloat16
SUB = 8
LANE = 128
SIDE = 4
LOG2E = math.log2(math.e)
OFFS = (0, -1, 1, 2)


def kernel_body(
    dims,
    tok_ref,
    gain_ref,
    w_in_hbm,
    w_low_hbm,
    w_dt_hbm,
    a_ref,
    bias_ref,
    skip_ref,
    thresh_ref,
    w_out_hbm,
    out_ref,
    raw,
    seld,
    w_in_v,
    w_low_v,
    w_dt_v,
    w_out_v,
    hid,
    agbuf,
    sqv,
    selp,
    arrecv,
    arres,
    expand_b,
    expand_c,
    bx,
    cx,
    step,
    cum,
    proj,
    yv,
    pin,
    ein,
    hst,
    hdev,
    hdec,
    esend_f,
    esend,
    erecv,
    tsend,
    trecv,
    gated,
    pbuf,
    x1,
    x2,
    s2,
    x3,
    x4,
    wsem,
    ag_s,
    ag_r,
    ar1_s,
    ar1_r,
    ar2_s,
    ar2_r,
    t_s,
    t_r,
    e_s,
    e_r,
    rs_s,
    rs_r,
):
    layers, n_seq, toks, feat, chans, states, rank = dims
    n_tp = SIDE * SIDE
    half = toks // 2
    quart = toks // 4
    eighth = toks // 8
    per_d = 2 * chans // LANE
    steps = toks // SUB
    arow = toks // n_tp
    ncb = chans // LANE
    seqi = lax.axis_index("seq")
    tpi = lax.axis_index("tp")
    zc = tpi // SIDE
    yc = lax.rem(tpi, SIDE)

    def wrap(v):
        return lax.rem(v + 2 * SIDE, SIDE)

    pos = ((yc, zc), (zc, yc))

    def blk(h, c1, c2):
        return c2 * SIDE + c1 if h == 0 else c1 * SIDE + c2

    def nb(h, axis, d):
        p1, p2 = pos[h]
        if axis == 1:
            return {"tp": blk(h, wrap(p1 + d), p2)}
        return {"tp": blk(h, p1, wrap(p2 + d))}

    def rcopy(src, dst, ssem, rsem, dev):
        return pltpu.make_async_remote_copy(
            src_ref=src, dst_ref=dst, send_sem=ssem, recv_sem=rsem,
            device_id=dev, device_id_type=MESH,
        )

    def wcopies(l):
        return (
            pltpu.make_async_copy(w_low_hbm.at[l], w_low_v.at[l, : rank + 2 * states], wsem.at[l, 0]),
            pltpu.make_async_copy(w_dt_hbm.at[l], w_dt_v.at[l], wsem.at[l, 1]),
            pltpu.make_async_copy(w_in_hbm.at[l], raw, wsem.at[l, 2]),
            pltpu.make_async_copy(w_out_hbm.at[l], w_out_v.at[l], wsem.at[l, 3]),
        )

    first_copies = wcopies(0)
    later_copies = wcopies(1)
    for c in (first_copies[0], first_copies[2], first_copies[1], first_copies[3],
              later_copies[0], later_copies[1], later_copies[3]):
        c.start()

    barrier = pltpu.get_barrier_semaphore()
    for d in range(1, n_tp):
        pl.semaphore_signal(barrier, inc=1, device_id={"tp": lax.rem(tpi + d, n_tp)}, device_id_type=MESH)
    for d in range(1, n_seq):
        pl.semaphore_signal(barrier, inc=1, device_id={"seq": lax.rem(seqi + d, n_seq)}, device_id_type=MESH)
    pl.semaphore_wait(barrier, n_tp + n_seq - 2)

    ri = lax.broadcasted_iota(jnp.int32, (toks, toks), 0)
    ci = lax.broadcasted_iota(jnp.int32, (toks, toks), 1)
    perm = jnp.where(ci == lax.rem(ri, SUB) * steps + ri // SUB, 1.0, 0.0).astype(BF16)
    hid[...] = jnp.dot(perm, tok_ref[...], preferred_element_type=F32).astype(BF16)

    def ag_info(u, h, k):
        p1, p2 = pos[h]
        r0 = u * half + h * quart
        full = pl.ds(r0, quart)
        lo = pl.ds(r0, eighth)
        hi = pl.ds(r0 + eighth, eighth)
        if k < 4:
            m = k
            ax = 1

            def at(d):
                return blk(h, wrap(p1 + d), p2)
        else:
            m = (k - 4) % 4
            o = OFFS[(k - 4) // 4]
            ax = 2

            def at(d):
                return blk(h, wrap(p1 + o), wrap(p2 + d))

        src_d, dst_d, rows, to = (
            (0, -1, full, 1),
            (0, 1, full, -1),
            (-1, -2, lo, 1),
            (1, 2, hi, -1),
        )[m]
        return at(src_d), at(dst_d), rows, nb(h, ax, to)

    def ag_send(u, h, k):
        src, _, rows, dev = ag_info(u, h, k)
        ref = agbuf.at[src, rows]
        return rcopy(ref, ref, ag_s.at[u, h, k], ag_r.at[u, h, k], dev)

    def ag_start(u, *ks):
        for k in ks:
            for h in range(2):
                ag_send(u, h, k).start()

    def ag_wait(u, *ks):
        for k in ks:
            for h in range(2):
                _, dst, rows, dev = ag_info(u, h, k)
                ref = agbuf.at[dst, rows]
                rcopy(ref, ref, ag_s.at[u, h, k], ag_r.at[u, h, k], dev).wait_recv()

    def publish(l, u):
        rows = pl.ds(u * half, half)
        own = hid[rows, :].astype(F32)
        gain_row = gain_ref[pl.ds(l, 1), pl.ds(pl.multiple_of(tpi * feat, feat), feat)]
        agbuf[tpi, rows] = (own * gain_row).astype(BF16)
        sqv[rows, :] = jnp.broadcast_to(jnp.sum(own * own, axis=1, keepdims=True), (half, LANE))
        ag_start(u, 0, 1, 4, 5)

    publish(0, 0)

    ei = lax.broadcasted_iota(jnp.int32, (LANE, states * LANE), 0)
    ej = lax.broadcasted_iota(jnp.int32, (LANE, states * LANE), 1) // LANE
    expand_b[...] = jnp.where(ei == ej, 1.0, 0.0).astype(BF16)
    expand_c[...] = jnp.where(ei == ej + states, 1.0, 0.0).astype(BF16)
    grp = 2 * LANE // per_d
    gi = lax.broadcasted_iota(jnp.int32, (2 * LANE, 2 * LANE), 0)
    gj = lax.broadcasted_iota(jnp.int32, (2 * LANE, 2 * LANE), 1)
    seld[...] = jnp.where(gj == lax.rem(gi, grp) * per_d + gi // grp, 1.0, 0.0).astype(BF16)
    sel_w = rank + LANE
    pad_from = rank + 2 * states
    for l in range(layers):
        w_low_v[l, pad_from:, :] = jnp.zeros((sel_w - pad_from, feat), BF16)

    def regroup(b0, b1):
        def one(i, unused):
            r = pl.multiple_of(i * 4 * LANE, 4 * LANE)
            two = jnp.concatenate(
                [raw[pl.ds(r, 2 * LANE), :], raw[pl.ds(r + 2 * LANE, 2 * LANE), :]], axis=1
            )
            got = jnp.dot(seld[...], two, preferred_element_type=F32).astype(BF16)
            d0 = pl.multiple_of(i * 2 * grp, 2 * grp)
            for q in range(per_d):
                cols = pl.ds((q % 2) * chans + (q // 2) * LANE, LANE)
                for v in range(2):
                    w_in_v[pl.ds(d0 + v * grp, grp), cols] = got[
                        q * grp : (q + 1) * grp, v * LANE : (v + 1) * LANE
                    ]
            return unused

        lax.fori_loop(b0, b1, one, 0)

    nreg = n_tp * feat // (2 * grp)

    def seq_copy(l, src, dst, ss, rs, q, sending):
        slot = seqi if sending else q
        return rcopy(src, dst.at[l, slot], ss.at[l, q], rs.at[l, slot], {"seq": q})

    def t_copy(l, q, sending):
        return seq_copy(l, tsend.at[l], trecv, t_s, t_r, q, sending)

    def e_copy(l, q, sending):
        return seq_copy(l, esend.at[l], erecv, e_s, e_r, q, sending)

    lo = pl.ds(0, eighth)
    hi = pl.ds(eighth, eighth)

    def rpos(h):
        p2, p1 = pos[h]
        return p1, p2

    def rnb(h, axis, d):
        return nb(h, 3 - axis, d)

    def rs_copy(u, h, k):
        p1, p2 = rpos(h)
        src, dst, dev = (
            lambda: (pbuf.at[u, h, wrap(p1 + 2), :, lo], x1.at[u, h, 0], rnb(h, 1, 1)),
            lambda: (pbuf.at[u, h, wrap(p1 + 2), :, hi], x1.at[u, h, 1], rnb(h, 1, -1)),
            lambda: (pbuf.at[u, h, wrap(p1 + 1)], x2.at[u, h, 0], rnb(h, 1, 1)),
            lambda: (pbuf.at[u, h, wrap(p1 - 1)], x2.at[u, h, 1], rnb(h, 1, -1)),
            lambda: (s2.at[u, h, wrap(p2 + 2), lo], x3.at[u, h, 0], rnb(h, 2, 1)),
            lambda: (s2.at[u, h, wrap(p2 + 2), hi], x3.at[u, h, 1], rnb(h, 2, -1)),
            lambda: (s2.at[u, h, wrap(p2 + 1)], x4.at[u, h, 0], rnb(h, 2, 1)),
            lambda: (s2.at[u, h, wrap(p2 - 1)], x4.at[u, h, 1], rnb(h, 2, -1)),
        )[k]()
        return rcopy(src, dst, rs_s.at[u, h, k], rs_r.at[u, h, k], dev)

    def omm(l, u, pairs):
        lhs = gated[u * half : (u + 1) * half, :]
        for dz, dy in pairs:
            z, y = wrap(zc + dz), wrap(yc + dy)
            cols = pl.ds(pl.multiple_of((z * SIDE + y) * feat, feat), feat)
            val = jnp.dot(lhs, w_out_v[l, :, cols], preferred_element_type=F32).astype(BF16)
            pbuf[u, 0, z, y] = val[:quart]
            pbuf[u, 1, y, z] = val[quart:]

    def rs1(l, u):
        omm(l, u, ((2, 0), (2, 1), (2, 2), (2, 3), (0, 2), (1, 2), (3, 2)))
        for h in range(2):
            rs_copy(u, h, 0).start()
            rs_copy(u, h, 1).start()

    def rs2(u):
        for h in range(2):
            p1, _ = rpos(h)
            up = wrap(p1 + 1)
            dn = wrap(p1 - 1)
            rs_copy(u, h, 0).wait_recv()
            pbuf[u, h, up, :, lo] = (
                pbuf[u, h, up, :, lo].astype(F32) + x1[u, h, 0].astype(F32)
            ).astype(BF16)
            rs_copy(u, h, 2).start()
            rs_copy(u, h, 1).wait_recv()
            pbuf[u, h, dn, :, hi] = (
                pbuf[u, h, dn, :, hi].astype(F32) + x1[u, h, 1].astype(F32)
            ).astype(BF16)
            rs_copy(u, h, 3).start()

    def sum3(u, h, p1, c2):
        return (
            pbuf[u, h, p1, c2].astype(F32) + x2[u, h, 0, c2].astype(F32) + x2[u, h, 1, c2].astype(F32)
        )

    def rs3(u):
        for h in range(2):
            p1, p2 = rpos(h)
            rs_copy(u, h, 2).wait_recv()
            rs_copy(u, h, 3).wait_recv()
            far = wrap(p2 + 2)
            s2[u, h, far] = sum3(u, h, p1, far).astype(BF16)
            rs_copy(u, h, 4).start()
            rs_copy(u, h, 5).start()
            for d in (1, -1):
                c2 = wrap(p2 + d)
                s2[u, h, c2] = sum3(u, h, p1, c2).astype(BF16)

    def rs4(u):
        for h in range(2):
            _, p2 = rpos(h)
            up = wrap(p2 + 1)
            dn = wrap(p2 - 1)
            rs_copy(u, h, 4).wait_recv()
            s2[u, h, up, lo] = (s2[u, h, up, lo].astype(F32) + x3[u, h, 0].astype(F32)).astype(BF16)
            rs_copy(u, h, 6).start()
            rs_copy(u, h, 5).wait_recv()
            s2[u, h, dn, hi] = (s2[u, h, dn, hi].astype(F32) + x3[u, h, 1].astype(F32)).astype(BF16)
            rs_copy(u, h, 7).start()

    def rs5(u):
        for h in range(2):
            p1, p2 = rpos(h)
            rs_copy(u, h, 6).wait_recv()
            rs_copy(u, h, 7).wait_recv()
            total = sum3(u, h, p1, p2) + x4[u, h, 0].astype(F32) + x4[u, h, 1].astype(F32)
            rows = pl.ds(u * half + h * quart, quart)
            hid[rows, :] = (hid[rows, :].astype(F32) + total).astype(BF16)

    def layer(l, unused):
        low_c, dt_c, in_c, out_c = wcopies(l)
        publish(l, 1)

        low_c.wait()
        selv = lax.dot_general(
            agbuf[tpi], w_low_v[l], (((1,), (1,)), ((), ())), preferred_element_type=F32
        )
        sq = sqv[:, 0:1]
        sq_hi = sq.astype(BF16).astype(F32)
        lane = lax.broadcasted_iota(jnp.int32, (toks, sel_w), 1)
        selv = jnp.where(lane == pad_from, sq_hi, selv)
        selv = jnp.where(lane == pad_from + 1, sq - sq_hi, selv)
        selp[...] = selv.astype(BF16)
        arrecv[tpi] = selp[pl.ds(pl.multiple_of(tpi * arow, arow), arow), :]

        def ar1(d, sending):
            to = lax.rem(tpi + d, n_tp)
            fr = lax.rem(tpi + n_tp - d, n_tp)
            rows = pl.ds(pl.multiple_of(to * arow, arow), arow)
            dst = arrecv.at[tpi] if sending else arrecv.at[fr]
            return rcopy(selp.at[rows], dst, ar1_s.at[d], ar1_r.at[d], {"tp": to})

        for d in range(1, n_tp):
            ar1(d, True).start()

        in_c.wait()
        ag_wait(0, 0, 1)
        ag_start(0, 2, 3, 8, 9, 12, 13)
        ag_wait(0, 4, 5)
        ag_start(0, 6, 7)
        regroup(0, nreg // 4)
        ag_wait(1, 0, 1)
        ag_start(1, 2, 3, 8, 9, 12, 13)
        ag_wait(0, 2, 3)
        ag_start(0, 16, 17)
        ag_wait(0, 8, 9)
        ag_start(0, 10, 11)
        ag_wait(0, 12, 13)
        ag_start(0, 14, 15)
        ag_wait(1, 4, 5)
        ag_start(1, 6, 7)

        for d in range(1, n_tp):
            ar1(d, False).wait_recv()
        tot = jnp.zeros((arow, sel_w), F32)
        for i in range(n_tp):
            tot = tot + arrecv[i].astype(F32)
        lane = lax.broadcasted_iota(jnp.int32, (arow, sel_w), 1)
        is_sq = (lane == pad_from) | (lane == pad_from + 1)
        ssum = jnp.sum(jnp.where(is_sq, tot, 0.0), axis=1, keepdims=True)
        factor = lax.rsqrt(ssum / (n_tp * feat) + 1e-05)
        f_hi = factor.astype(BF16).astype(F32)
        tot = jnp.where(lane == pad_from, f_hi, jnp.where(lane == pad_from + 1, factor - f_hi, tot * factor))
        mine = pl.ds(pl.multiple_of(tpi * arow, arow), arow)
        arres[mine, :] = tot.astype(BF16)

        def ar2(d, sending):
            to = lax.rem(tpi + d, n_tp)
            fr = lax.rem(tpi + n_tp - d, n_tp)
            base = tpi if sending else fr
            rows = pl.ds(pl.multiple_of(base * arow, arow), arow)
            return rcopy(arres.at[rows], arres.at[rows], ar2_s.at[d], ar2_r.at[d], {"tp": to})

        for d in range(1, n_tp):
            ar2(d, True).start()

        regroup(nreg // 4, nreg // 2)
        ag_wait(1, 2, 3)
        ag_start(1, 16, 17)
        ag_wait(0, 16, 17)
        ag_start(0, 18, 19)
        ag_wait(1, 8, 9)
        ag_start(1, 10, 11)
        ag_wait(1, 12, 13)
        ag_start(1, 14, 15)
        regroup(nreg // 2, nreg)

        @pl.when(l + 1 < layers)
        def _():
            later_copies[2].start()

        for d in range(1, n_tp):
            ar2(d, False).wait_recv()
        tail = arres[:, rank:]
        tl = lax.broadcasted_iota(jnp.int32, (toks, LANE), 1)
        in_f = (tl == 2 * states) | (tl == 2 * states + 1)
        fac = jnp.sum(jnp.where(in_f, tail.astype(F32), 0.0), axis=1, keepdims=True)
        dt_c.wait()
        pre = jnp.dot(arres[:, :rank], w_dt_v[l], preferred_element_type=F32) + bias_ref[pl.ds(l, 1), :]
        step[...] = jnp.maximum(pre, 0.0) + jnp.log1p(jnp.exp(-jnp.abs(pre)))
        bx[...] = jnp.dot(tail, expand_b[...], preferred_element_type=F32)
        cx[...] = jnp.dot(tail, expand_c[...], preferred_element_type=F32)

        def accum(t, run):
            rows = pl.ds(pl.multiple_of(t * SUB, SUB), SUB)
            run = run + step[rows, :]
            cum[rows, :] = run
            return run

        ctot = lax.fori_loop(0, steps, accum, jnp.zeros((SUB, chans), F32))
        tsend[l] = jnp.broadcast_to(jnp.sum(ctot, axis=0, keepdims=True), (SUB, chans))
        for q in range(1, n_seq):
            @pl.when(q > seqi)
            def _():
                t_copy(l, q, True).start()

        skip_row = skip_ref[pl.ds(l, 1), :]
        th_row = thresh_ref[pl.ds(l, 1), :]

        def mm(u, first, pairs):
            rs = pl.ds(u * half, half)
            for i, (dz, dy) in enumerate(pairs):
                b = wrap(zc + dz) * SIDE + wrap(yc + dy)
                rows = pl.ds(pl.multiple_of(b * feat, feat), feat)
                val = jnp.dot(agbuf[b, rs], w_in_v[rows, :], preferred_element_type=F32)
                if first and i == 0:
                    proj[rs, :] = val
                else:
                    proj[rs, :] += val

        near = ((0, 0), (0, 1), (0, -1), (1, 0), (-1, 0), (1, 1), (1, -1), (-1, 1), (-1, -1))
        away = ((2, 0), (2, 1), (2, 2), (2, 3), (0, 2), (1, 2), (3, 2))

        def scan(u):
            for cb in range(ncb):
                cs = pl.ds(cb * LANE, LANE)
                na = [
                    jnp.broadcast_to(a_ref[l, s : s + 1, cs] * (-LOG2E), (SUB, LANE))
                    for s in range(states)
                ]
                skip = skip_row[:, cb * LANE : (cb + 1) * LANE]

                def scan_step(t, hs):
                    rows = pl.ds(pl.multiple_of(t * SUB, SUB), SUB)
                    st = step[rows, cs]
                    cur = proj[rows, cs]
                    dr = st * cur
                    acc = skip * cur
                    new = []
                    for s in range(states):
                        ls = pl.ds(s * LANE, LANE)
                        hn = jnp.exp2(st * na[s]) * hs[s] + bx[rows, ls] * dr
                        acc = acc + cx[rows, ls] * hn
                        new.append(hn)
                    yv[rows, cs] = acc
                    return tuple(new)

                if u == 0:
                    init = tuple(jnp.zeros((SUB, LANE), F32) for _ in range(states))
                else:
                    init = tuple(hst[s, :, cs] for s in range(states))
                hs = lax.fori_loop(u * steps // 2, (u + 1) * steps // 2, scan_step, init)
                if u == 0:
                    for s in range(states):
                        hst[s, :, cs] = hs[s]
                    continue
                sub = lax.broadcasted_iota(jnp.int32, (SUB, LANE), 0)
                ct = cum[pl.ds((steps - 1) * SUB, SUB), cs]
                for s in range(states):
                    e = hs[s]
                    p = jnp.exp2(ct * na[s])
                    for d in (1, 2, 4):
                        ok = sub >= d
                        e = e + jnp.where(ok, p * pltpu.roll(e, d, 0), 0.0)
                        p = p * jnp.where(ok, pltpu.roll(p, d, 0), 1.0)
                    esend_f[s : s + 1, cs] = e[SUB - 1 : SUB, :]
                    ein[s, :, cs] = jnp.where(sub >= 1, pltpu.roll(e, 1, 0), 0.0)
                    pin[s, :, cs] = jnp.where(sub >= 1, pltpu.roll(p, 1, 0), 1.0)

        ag_wait(1, 16, 17)
        ag_start(1, 18, 19)
        ag_wait(0, 6, 7, 10, 11, 14, 15, 18, 19)
        mm(0, True, near + away)
        proj[:half, :] = proj[:half, :] * fac[:half]
        scan(0)
        mm(1, True, near)
        ag_wait(1, 6, 7, 10, 11, 14, 15, 18, 19)
        mm(1, False, away)
        proj[half:, :] = proj[half:, :] * fac[half:]
        scan(1)

        esend[l] = esend_f[...].astype(BF16)
        for q in range(1, n_seq):
            @pl.when(q > seqi)
            def _():
                e_copy(l, q, True).start()

        for u in range(2):
            for k in range(20):
                for h in range(2):
                    ag_send(u, h, k).wait_send()
        for d in range(1, n_tp):
            ar1(d, True).wait_send()
            ar2(d, True).wait_send()

        rates = a_ref[l] * (-LOG2E)
        for q in range(n_seq - 1):
            @pl.when(q < seqi)
            def _():
                t_copy(l, q, False).wait_recv()
                hdec[q] = jnp.exp2(rates * trecv[l, q, 0:1, :])

        hdev[...] = jnp.zeros_like(hdev)
        for q in range(n_seq - 1):
            @pl.when(q < seqi)
            def _():
                e_copy(l, q, False).wait_recv()
                hdev[...] = hdec[q] * hdev[...] + erecv[l, q].astype(F32)

        def finish(u):
            rs = pl.ds(u * half, half)
            for cb in range(ncb):
                cs = pl.ds(cb * LANE, LANE)
                na = [
                    jnp.broadcast_to(a_ref[l, s : s + 1, cs] * (-LOG2E), (SUB, LANE))
                    for s in range(states)
                ]
                hin = [ein[s, :, cs] + pin[s, :, cs] * hdev[s : s + 1, cs] for s in range(states)]
                th = th_row[:, cb * LANE : (cb + 1) * LANE]

                def fold(t, unused):
                    rows = pl.ds(pl.multiple_of(t * SUB, SUB), SUB)
                    ct = cum[rows, cs]
                    acc = yv[rows, cs]
                    for s in range(states):
                        ls = pl.ds(s * LANE, LANE)
                        acc = acc + cx[rows, ls] * (jnp.exp2(ct * na[s]) * hin[s])
                    yv[rows, cs] = acc
                    return unused

                lax.fori_loop(u * steps // 2, (u + 1) * steps // 2, fold, 0)

                mixed = yv[rs, cs]
                fct = lax.rsqrt(jnp.mean(mixed * mixed, axis=1, keepdims=True) + 1e-05)
                normal = mixed * fct
                shrunk = jnp.maximum(normal - th, 0.0) - jnp.maximum(-normal - th, 0.0)
                gate = proj[rs, pl.ds(chans + cb * LANE, LANE)]
                gated[rs, cs] = (shrunk * (gate / (1.0 + jnp.exp(-gate)))).astype(BF16)

        others = ((0, 0), (0, 1), (0, -1), (1, 0), (-1, 0), (1, 1), (1, -1), (-1, 1), (-1, -1))
        finish(0)
        out_c.wait()
        rs1(l, 0)
        omm(l, 0, others)
        finish(1)
        rs1(l, 1)
        rs2(0)
        omm(l, 1, others)
        rs2(1)
        rs3(0)
        rs4(0)
        rs3(1)
        rs5(0)

        @pl.when(l + 1 < layers)
        def _():
            publish(l + 1, 0)

        rs4(1)
        rs5(1)
        for u in range(2):
            for h in range(2):
                for k in range(8):
                    rs_copy(u, h, k).wait_send()
        for q in range(1, n_seq):
            @pl.when(q > seqi)
            def _():
                t_copy(l, q, True).wait_send()
                e_copy(l, q, True).wait_send()
        return unused

    lax.fori_loop(0, layers, layer, 0)
    out_ref[...] = lax.dot_general(
        perm, hid[...], (((0,), (0,)), ((), ())), preferred_element_type=F32
    ).astype(BF16)


def per_device(n_seq, tokens, norm_gain, w_in, w_low, w_dt, a_rate, dt_bias, skip_gain, threshold, w_out):
    toks, feat = tokens.shape
    layers, model, _, chans = w_in.shape
    states = a_rate.shape[1]
    rank = w_dt.shape[1]
    n_tp = SIDE * SIDE
    half, quart, eighth = toks // 2, toks // 4, toks // 8
    per_d = 2 * chans // LANE
    sel_w = rank + LANE
    dims = (layers, n_seq, toks, feat, chans, states, rank)
    vm = pl.BlockSpec(memory_space=pltpu.VMEM)
    hb = pl.BlockSpec(memory_space=pl.ANY)
    dma = pltpu.SemaphoreType.DMA
    V = pltpu.VMEM
    return pl.pallas_call(
        functools.partial(kernel_body, dims),
        out_shape=jax.ShapeDtypeStruct((toks, feat), BF16),
        in_specs=[vm, vm, hb, hb, hb, vm, vm, vm, vm, hb],
        out_specs=vm,
        scratch_shapes=[
            V((model * per_d, LANE), BF16),
            V((2 * LANE, 2 * LANE), BF16),
            V((model, 2 * chans), BF16),
            V((layers, sel_w, feat), BF16),
            V((layers, rank, chans), BF16),
            V((layers, chans, model), BF16),
            V((toks, feat), BF16),
            V((n_tp, toks, feat), BF16),
            V((toks, LANE), F32),
            V((toks, sel_w), BF16),
            V((n_tp, toks // n_tp, sel_w), BF16),
            V((toks, sel_w), BF16),
            V((LANE, states * LANE), BF16),
            V((LANE, states * LANE), BF16),
            V((toks, states * LANE), F32),
            V((toks, states * LANE), F32),
            V((toks, chans), F32),
            V((toks, chans), F32),
            V((toks, 2 * chans), F32),
            V((toks, chans), F32),
            V((states, SUB, chans), F32),
            V((states, SUB, chans), F32),
            V((states, SUB, chans), F32),
            V((states, chans), F32),
            V((n_seq, states, chans), F32),
            V((states, chans), F32),
            V((layers, states, chans), BF16),
            V((layers, n_seq, states, chans), BF16),
            V((layers, SUB, chans), F32),
            V((layers, n_seq, SUB, chans), F32),
            V((toks, chans), BF16),
            V((2, 2, SIDE, SIDE, quart, feat), BF16),
            V((2, 2, 2, SIDE, eighth, feat), BF16),
            V((2, 2, 2, SIDE, quart, feat), BF16),
            V((2, 2, SIDE, quart, feat), BF16),
            V((2, 2, 2, eighth, feat), BF16),
            V((2, 2, 2, quart, feat), BF16),
            dma((layers, 4)),
            dma((2, 2, 20)),
            dma((2, 2, 20)),
            dma((n_tp,)),
            dma((n_tp,)),
            dma((n_tp,)),
            dma((n_tp,)),
            dma((layers, n_seq)),
            dma((layers, n_seq)),
            dma((layers, n_seq)),
            dma((layers, n_seq)),
            dma((2, 2, 8)),
            dma((2, 2, 8)),
        ],
        compiler_params=pltpu.CompilerParams(
            collective_id=0, has_side_effects=True, vmem_limit_bytes=60 * 1024 * 1024
        ),
    )(
        tokens,
        norm_gain,
        jnp.swapaxes(w_in.reshape(layers, model, 2, chans // LANE, LANE), 2, 3).reshape(
            layers, model * per_d, LANE
        ),
        jnp.swapaxes(w_low, 1, 2),
        w_dt,
        a_rate,
        dt_bias,
        skip_gain,
        threshold,
        w_out,
    )


def solution(mesh):
    in_specs = (
        P("seq", "tp"),
        P(),
        P(None, None, None, "tp"),
        P(None, "tp", None),
        P(None, None, "tp"),
        P(None, None, "tp"),
        P(None, "tp"),
        P(None, "tp"),
        P(None, "tp"),
        P(None, "tp", None),
    )
    return jax.shard_map(
        functools.partial(per_device, mesh.shape["seq"]),
        mesh=mesh,
        in_specs=in_specs,
        out_specs=P("seq", "tp"),
        check_vma=False,
    )
```

time: 151 us -> 123 us (0.81)
  local copies, waits for them, and re-layouts: 28.9 us -> 1.57 us
    reshape x1 -> x0, local copies, waits for them, and re-layouts: 27.3 us -> none  [per_device(): w_in.reshape(layers, model, 2 * chans)]
where the time goes in v1:
time: 123 us
  Pallas kernels  121 us (98%)
  local copies, waits for them, and re-layouts  1.57 us (1%)
    pallas_call x1, Pallas kernels, per_device(): pl.pallas_call(functools.partial(kernel_body, dims), out_shape=jax.ShapeD...  121 us

profile of v1, /device:TPU:6, one launch (start us, length us, event | category | flops | bytes accessed | tf_op | source)
XLA Modules:
  0.0 122.9 jit_solution(7939105151619326887)
XLA Ops:
  0.0 121.3 %shard_map.100 = bf16[256,256]{1,0:T(8,128)(2,1)} custom-call(bf16[256,256]{1,0:T(8,128)(2,1)} %tok_ref.1, f32[2,4096]{1,0:T(2,128)} %gain_ref.1, bf16[2,32768,128]{2,1,0:T(8,128)(2,1)} %bitcast.6, bf16[2,288,256]{2,1,0:T(8,128)(2,1)} %bitcast.7, bf16[2,256,512]{2,1,0:T(8,128)(2,1)} %w_dt_hbm.1, f32[2,16,512]{2,1,0:T(8,128)} %a_ref.1, f32[2,512]{1,0:T(2,128)} %bias_ref.1, ...), custom_call_target="tpu_custom_call" | custom-call | tf_op jit(solution)/shard_map/pallas_call | solution.py:629
  121.3 1.6 %copy.13 = bf16[256,256]{1,0:T(8,128)(2,1)} copy(bf16[256,256]{1,0:T(8,128)(2,1)} %shard_map.100) | data formatting | bytes 262144

commit v2 on v1

--- a/solution.py
+++ b/solution.py
@@ -16,6 +16,8 @@
 SIDE = 4
 LOG2E = math.log2(math.e)
 OFFS = (0, -1, 1, 2)
+WIDE = 8
+AG_KEYS = (0, 1, 2) + tuple(range(4, 20))
 
 
 def kernel_body(
@@ -67,7 +69,6 @@
     x2,
     s2,
     x3,
-    x4,
     wsem,
     ag_s,
     ag_r,
@@ -149,25 +150,24 @@
         lo = pl.ds(r0, eighth)
         hi = pl.ds(r0 + eighth, eighth)
         if k < 4:
-            m = k
-            ax = 1
+            to = (1, -1, 2)[k]
+            src_d, dst_d, rows, ax = 0, -to, full, 1
 
             def at(d):
                 return blk(h, wrap(p1 + d), p2)
         else:
-            m = (k - 4) % 4
+            src_d, dst_d, rows, to = (
+                (0, -1, full, 1),
+                (0, 1, full, -1),
+                (-1, -2, lo, 1),
+                (1, 2, hi, -1),
+            )[(k - 4) % 4]
             o = OFFS[(k - 4) // 4]
             ax = 2
 
             def at(d):
                 return blk(h, wrap(p1 + o), wrap(p2 + d))
 
-        src_d, dst_d, rows, to = (
-            (0, -1, full, 1),
-            (0, 1, full, -1),
-            (-1, -2, lo, 1),
-            (1, 2, hi, -1),
-        )[m]
         return at(src_d), at(dst_d), rows, nb(h, ax, to)
 
     def ag_send(u, h, k):
@@ -193,7 +193,7 @@
         gain_row = gain_ref[pl.ds(l, 1), pl.ds(pl.multiple_of(tpi * feat, feat), feat)]
         agbuf[tpi, rows] = (own * gain_row).astype(BF16)
         sqv[rows, :] = jnp.broadcast_to(jnp.sum(own * own, axis=1, keepdims=True), (half, LANE))
-        ag_start(u, 0, 1, 4, 5)
+        ag_start(u, 0, 1, 4, 5, 2)
 
     publish(0, 0)
 
@@ -212,15 +212,15 @@
 
     def regroup(b0, b1):
         def one(i, unused):
-            r = pl.multiple_of(i * 4 * LANE, 4 * LANE)
-            two = jnp.concatenate(
-                [raw[pl.ds(r, 2 * LANE), :], raw[pl.ds(r + 2 * LANE, 2 * LANE), :]], axis=1
-            )
-            got = jnp.dot(seld[...], two, preferred_element_type=F32).astype(BF16)
-            d0 = pl.multiple_of(i * 2 * grp, 2 * grp)
+            r = pl.multiple_of(i * WIDE * 2 * LANE, WIDE * 2 * LANE)
+            parts = [raw[pl.ds(r + v * 2 * LANE, 2 * LANE), :] for v in range(WIDE)]
+            got = jnp.dot(
+                seld[...], jnp.concatenate(parts, axis=1), preferred_element_type=F32
+            ).astype(BF16)
+            d0 = pl.multiple_of(i * WIDE * grp, WIDE * grp)
             for q in range(per_d):
                 cols = pl.ds((q % 2) * chans + (q // 2) * LANE, LANE)
-                for v in range(2):
+                for v in range(WIDE):
                     w_in_v[pl.ds(d0 + v * grp, grp), cols] = got[
                         q * grp : (q + 1) * grp, v * LANE : (v + 1) * LANE
                     ]
@@ -228,7 +228,7 @@
 
         lax.fori_loop(b0, b1, one, 0)
 
-    nreg = n_tp * feat // (2 * grp)
+    nreg = n_tp * feat // (WIDE * grp)
 
     def seq_copy(l, src, dst, ss, rs, q, sending):
         slot = seqi if sending else q
@@ -257,10 +257,9 @@
             lambda: (pbuf.at[u, h, wrap(p1 + 2), :, hi], x1.at[u, h, 1], rnb(h, 1, -1)),
             lambda: (pbuf.at[u, h, wrap(p1 + 1)], x2.at[u, h, 0], rnb(h, 1, 1)),
             lambda: (pbuf.at[u, h, wrap(p1 - 1)], x2.at[u, h, 1], rnb(h, 1, -1)),
-            lambda: (s2.at[u, h, wrap(p2 + 2), lo], x3.at[u, h, 0], rnb(h, 2, 1)),
-            lambda: (s2.at[u, h, wrap(p2 + 2), hi], x3.at[u, h, 1], rnb(h, 2, -1)),
-            lambda: (s2.at[u, h, wrap(p2 + 1)], x4.at[u, h, 0], rnb(h, 2, 1)),
-            lambda: (s2.at[u, h, wrap(p2 - 1)], x4.at[u, h, 1], rnb(h, 2, -1)),
+            lambda: (s2.at[u, h, wrap(p2 + 1)], x3.at[u, h, 0], rnb(h, 2, 1)),
+            lambda: (s2.at[u, h, wrap(p2 - 1)], x3.at[u, h, 1], rnb(h, 2, -1)),
+            lambda: (s2.at[u, h, wrap(p2 + 2)], x3.at[u, h, 2], rnb(h, 2, 2)),
         )[k]()
         return rcopy(src, dst, rs_s.at[u, h, k], rs_r.at[u, h, k], dev)
 
@@ -305,32 +304,18 @@
             p1, p2 = rpos(h)
             rs_copy(u, h, 2).wait_recv()
             rs_copy(u, h, 3).wait_recv()
-            far = wrap(p2 + 2)
-            s2[u, h, far] = sum3(u, h, p1, far).astype(BF16)
-            rs_copy(u, h, 4).start()
-            rs_copy(u, h, 5).start()
-            for d in (1, -1):
+            for k, d in ((6, 2), (4, 1), (5, -1)):
                 c2 = wrap(p2 + d)
                 s2[u, h, c2] = sum3(u, h, p1, c2).astype(BF16)
+                rs_copy(u, h, k).start()
 
     def rs4(u):
         for h in range(2):
-            _, p2 = rpos(h)
-            up = wrap(p2 + 1)
-            dn = wrap(p2 - 1)
-            rs_copy(u, h, 4).wait_recv()
-            s2[u, h, up, lo] = (s2[u, h, up, lo].astype(F32) + x3[u, h, 0].astype(F32)).astype(BF16)
-            rs_copy(u, h, 6).start()
-            rs_copy(u, h, 5).wait_recv()
-            s2[u, h, dn, hi] = (s2[u, h, dn, hi].astype(F32) + x3[u, h, 1].astype(F32)).astype(BF16)
-            rs_copy(u, h, 7).start()
-
-    def rs5(u):
-        for h in range(2):
             p1, p2 = rpos(h)
-            rs_copy(u, h, 6).wait_recv()
-            rs_copy(u, h, 7).wait_recv()
-            total = sum3(u, h, p1, p2) + x4[u, h, 0].astype(F32) + x4[u, h, 1].astype(F32)
+            total = sum3(u, h, p1, p2)
+            for k in range(3):
+                rs_copy(u, h, 4 + k).wait_recv()
+                total = total + x3[u, h, k].astype(F32)
             rows = pl.ds(u * half + h * quart, quart)
             hid[rows, :] = (hid[rows, :].astype(F32) + total).astype(BF16)
 
@@ -360,22 +345,33 @@
         for d in range(1, n_tp):
             ar1(d, True).start()
 
-        in_c.wait()
+        @pl.when(l == 0)
+        def _():
+            in_c.wait()
+
         ag_wait(0, 0, 1)
-        ag_start(0, 2, 3, 8, 9, 12, 13)
+        ag_start(0, 8, 9, 12, 13)
         ag_wait(0, 4, 5)
         ag_start(0, 6, 7)
-        regroup(0, nreg // 4)
+        ag_wait(0, 2)
+        ag_start(0, 16, 17)
+
+        @pl.when(l == 0)
+        def _():
+            regroup(0, nreg // 4)
+
         ag_wait(1, 0, 1)
-        ag_start(1, 2, 3, 8, 9, 12, 13)
-        ag_wait(0, 2, 3)
-        ag_start(0, 16, 17)
+        ag_start(1, 8, 9, 12, 13)
+        ag_wait(1, 4, 5)
+        ag_start(1, 6, 7)
+        ag_wait(1, 2)
+        ag_start(1, 16, 17)
         ag_wait(0, 8, 9)
         ag_start(0, 10, 11)
         ag_wait(0, 12, 13)
         ag_start(0, 14, 15)
-        ag_wait(1, 4, 5)
-        ag_start(1, 6, 7)
+        ag_wait(0, 16, 17)
+        ag_start(0, 18, 19)
 
         for d in range(1, n_tp):
             ar1(d, False).wait_recv()
@@ -401,19 +397,20 @@
         for d in range(1, n_tp):
             ar2(d, True).start()
 
-        regroup(nreg // 4, nreg // 2)
-        ag_wait(1, 2, 3)
-        ag_start(1, 16, 17)
-        ag_wait(0, 16, 17)
-        ag_start(0, 18, 19)
+        @pl.when(l == 0)
+        def _():
+            regroup(nreg // 4, nreg // 2)
+
         ag_wait(1, 8, 9)
         ag_start(1, 10, 11)
         ag_wait(1, 12, 13)
         ag_start(1, 14, 15)
-        regroup(nreg // 2, nreg)
-
-        @pl.when(l + 1 < layers)
+        ag_wait(1, 16, 17)
+        ag_start(1, 18, 19)
+
+        @pl.when(l == 0)
         def _():
+            regroup(nreg // 2, nreg)
             later_copies[2].start()
 
         for d in range(1, n_tp):
@@ -486,7 +483,7 @@
                     init = tuple(jnp.zeros((SUB, LANE), F32) for _ in range(states))
                 else:
                     init = tuple(hst[s, :, cs] for s in range(states))
-                hs = lax.fori_loop(u * steps // 2, (u + 1) * steps // 2, scan_step, init)
+                hs = lax.fori_loop(u * steps // 2, (u + 1) * steps // 2, scan_step, init, unroll=2)
                 if u == 0:
                     for s in range(states):
                         hst[s, :, cs] = hs[s]
@@ -504,8 +501,6 @@
                     ein[s, :, cs] = jnp.where(sub >= 1, pltpu.roll(e, 1, 0), 0.0)
                     pin[s, :, cs] = jnp.where(sub >= 1, pltpu.roll(p, 1, 0), 1.0)
 
-        ag_wait(1, 16, 17)
-        ag_start(1, 18, 19)
         ag_wait(0, 6, 7, 10, 11, 14, 15, 18, 19)
         mm(0, True, near + away)
         proj[:half, :] = proj[:half, :] * fac[:half]
@@ -523,7 +518,7 @@
                 e_copy(l, q, True).start()
 
         for u in range(2):
-            for k in range(20):
+            for k in AG_KEYS:
                 for h in range(2):
                     ag_send(u, h, k).wait_send()
         for d in range(1, n_tp):
@@ -544,9 +539,9 @@
                 e_copy(l, q, False).wait_recv()
                 hdev[...] = hdec[q] * hdev[...] + erecv[l, q].astype(F32)
 
-        def finish(u):
+        def finish(u, c0, c1):
             rs = pl.ds(u * half, half)
-            for cb in range(ncb):
+            for cb in range(c0, c1):
                 cs = pl.ds(cb * LANE, LANE)
                 na = [
                     jnp.broadcast_to(a_ref[l, s : s + 1, cs] * (-LOG2E), (SUB, LANE))
@@ -565,7 +560,7 @@
                     yv[rows, cs] = acc
                     return unused
 
-                lax.fori_loop(u * steps // 2, (u + 1) * steps // 2, fold, 0)
+                lax.fori_loop(u * steps // 2, (u + 1) * steps // 2, fold, 0, unroll=4)
 
                 mixed = yv[rs, cs]
                 fct = lax.rsqrt(jnp.mean(mixed * mixed, axis=1, keepdims=True) + 1e-05)
@@ -575,29 +570,40 @@
                 gated[rs, cs] = (shrunk * (gate / (1.0 + jnp.exp(-gate)))).astype(BF16)
 
         others = ((0, 0), (0, 1), (0, -1), (1, 0), (-1, 0), (1, 1), (1, -1), (-1, 1), (-1, -1))
-        finish(0)
+        finish(0, 0, ncb)
         out_c.wait()
         rs1(l, 0)
         omm(l, 0, others)
-        finish(1)
+        finish(1, 0, ncb // 2)
+        rs2(0)
+        finish(1, ncb // 2, ncb)
         rs1(l, 1)
-        rs2(0)
         omm(l, 1, others)
+
+        @pl.when(l + 1 < layers)
+        def _():
+            later_copies[2].wait()
+            regroup(0, nreg // 4)
+
         rs2(1)
         rs3(0)
+
+        @pl.when(l + 1 < layers)
+        def _():
+            regroup(nreg // 4, nreg // 2)
+
         rs4(0)
-        rs3(1)
-        rs5(0)
 
         @pl.when(l + 1 < layers)
         def _():
             publish(l + 1, 0)
-
+            regroup(nreg // 2, nreg)
+
+        rs3(1)
         rs4(1)
-        rs5(1)
         for u in range(2):
             for h in range(2):
-                for k in range(8):
+                for k in range(7):
                     rs_copy(u, h, k).wait_send()
         for q in range(1, n_seq):
             @pl.when(q > seqi)
@@ -667,8 +673,7 @@
             V((2, 2, 2, SIDE, eighth, feat), BF16),
             V((2, 2, 2, SIDE, quart, feat), BF16),
             V((2, 2, SIDE, quart, feat), BF16),
-            V((2, 2, 2, eighth, feat), BF16),
-            V((2, 2, 2, quart, feat), BF16),
+            V((2, 2, 3, quart, feat), BF16),
             dma((layers, 4)),
             dma((2, 2, 20)),
             dma((2, 2, 20)),

time: 123 us -> 115 us (0.935)
  Pallas kernels: 121 us -> 113 us
    pallas_call x1, Pallas kernels: 121 us -> 113 us  [per_device(): pl.pallas_call(functools.partial(kernel_body, dims), out_shape=jax.ShapeD...]
where the time goes in v2:
time: 115 us; the launch traced here: 114 us
  Pallas kernels  113 us (98%)
  local copies, waits for them, and re-layouts  1.57 us (1%)
    pallas_call x1, Pallas kernels, per_device(): pl.pallas_call(functools.partial(kernel_body, dims), out_shape=jax.ShapeD...  113 us

profile of v2, /device:TPU:6, one launch (start us, length us, event | category | flops | bytes accessed | tf_op | source)
XLA Modules:
  0.0 114.4 jit_solution(16397652165156115606)
XLA Ops:
  0.0 112.8 %shard_map.100 = bf16[256,256]{1,0:T(8,128)(2,1)} custom-call(bf16[256,256]{1,0:T(8,128)(2,1)} %tok_ref.1, f32[2,4096]{1,0:T(2,128)} %gain_ref.1, bf16[2,32768,128]{2,1,0:T(8,128)(2,1)} %bitcast.6, bf16[2,288,256]{2,1,0:T(8,128)(2,1)} %bitcast.7, bf16[2,256,512]{2,1,0:T(8,128)(2,1)} %w_dt_hbm.1, f32[2,16,512]{2,1,0:T(8,128)} %a_ref.1, f32[2,512]{1,0:T(2,128)} %bias_ref.1, ...), custom_call_target="tpu_custom_call" | custom-call | tf_op jit(solution)/shard_map/pallas_call | solution.py:635
  112.8 1.6 %copy.13 = bf16[256,256]{1,0:T(8,128)(2,1)} copy(bf16[256,256]{1,0:T(8,128)(2,1)} %shard_map.100) | data formatting | bytes 262144

commit v3 on v2

--- a/solution.py
+++ b/solution.py
@@ -16,6 +16,7 @@
 SIDE = 4
 LOG2E = math.log2(math.e)
 OFFS = (0, -1, 1, 2)
+OUT = (2, 1, -1, 0)
 WIDE = 8
 AG_KEYS = (0, 1, 2) + tuple(range(4, 20))
 
@@ -127,8 +128,7 @@
 
     first_copies = wcopies(0)
     later_copies = wcopies(1)
-    for c in (first_copies[0], first_copies[2], first_copies[1], first_copies[3],
-              later_copies[0], later_copies[1], later_copies[3]):
+    for c in (first_copies[0], first_copies[2]):
         c.start()
 
     barrier = pltpu.get_barrier_semaphore()
@@ -250,17 +250,24 @@
     def rnb(h, axis, d):
         return nb(h, 3 - axis, d)
 
+    ahead, up, down, here = range(SIDE)
+    parts = (pl.ds(0, 2), pl.ds(2, 2))
+
     def rs_copy(u, h, k):
-        p1, p2 = rpos(h)
-        src, dst, dev = (
-            lambda: (pbuf.at[u, h, wrap(p1 + 2), :, lo], x1.at[u, h, 0], rnb(h, 1, 1)),
-            lambda: (pbuf.at[u, h, wrap(p1 + 2), :, hi], x1.at[u, h, 1], rnb(h, 1, -1)),
-            lambda: (pbuf.at[u, h, wrap(p1 + 1)], x2.at[u, h, 0], rnb(h, 1, 1)),
-            lambda: (pbuf.at[u, h, wrap(p1 - 1)], x2.at[u, h, 1], rnb(h, 1, -1)),
-            lambda: (s2.at[u, h, wrap(p2 + 1)], x3.at[u, h, 0], rnb(h, 2, 1)),
-            lambda: (s2.at[u, h, wrap(p2 - 1)], x3.at[u, h, 1], rnb(h, 2, -1)),
-            lambda: (s2.at[u, h, wrap(p2 + 2)], x3.at[u, h, 2], rnb(h, 2, 2)),
-        )[k]()
+        if k < 8:
+            piece = parts[(k // 2) % 2]
+            way = k % 2
+            if k < 4:
+                src = pbuf.at[u, h, ahead, piece, (lo, hi)[way]]
+                dst = x1.at[u, h, way, piece]
+            else:
+                src = pbuf.at[u, h, (up, down)[way], piece]
+                dst = x2.at[u, h, way, piece]
+            dev = rnb(h, 1, (1, -1)[way])
+        else:
+            src = s2.at[u, h, (ahead, up, down)[k - 8]]
+            dst = x3.at[u, h, k - 8]
+            dev = rnb(h, 2, OUT[k - 8])
         return rcopy(src, dst, rs_s.at[u, h, k], rs_r.at[u, h, k], dev)
 
     def omm(l, u, pairs):
@@ -269,52 +276,54 @@
             z, y = wrap(zc + dz), wrap(yc + dy)
             cols = pl.ds(pl.multiple_of((z * SIDE + y) * feat, feat), feat)
             val = jnp.dot(lhs, w_out_v[l, :, cols], preferred_element_type=F32).astype(BF16)
-            pbuf[u, 0, z, y] = val[:quart]
-            pbuf[u, 1, y, z] = val[quart:]
+            iz, iy = OUT.index(dz), OUT.index(dy)
+            pbuf[u, 0, iz, iy] = val[:quart]
+            pbuf[u, 1, iy, iz] = val[quart:]
 
     def rs1(l, u):
-        omm(l, u, ((2, 0), (2, 1), (2, 2), (2, 3), (0, 2), (1, 2), (3, 2)))
+        omm(l, u, ((2, 2), (2, 1), (1, 2)))
         for h in range(2):
             rs_copy(u, h, 0).start()
             rs_copy(u, h, 1).start()
+        omm(l, u, ((2, -1), (2, 0), (-1, 2), (0, 2)))
+        for h in range(2):
+            rs_copy(u, h, 2).start()
+            rs_copy(u, h, 3).start()
+        omm(l, u, ((1, 1), (1, -1), (1, 0), (-1, 1), (-1, -1), (-1, 0), (0, 1), (0, -1)))
+        omm(l, u, ((0, 0),))
 
     def rs2(u):
-        for h in range(2):
-            p1, _ = rpos(h)
-            up = wrap(p1 + 1)
-            dn = wrap(p1 - 1)
-            rs_copy(u, h, 0).wait_recv()
-            pbuf[u, h, up, :, lo] = (
-                pbuf[u, h, up, :, lo].astype(F32) + x1[u, h, 0].astype(F32)
-            ).astype(BF16)
-            rs_copy(u, h, 2).start()
-            rs_copy(u, h, 1).wait_recv()
-            pbuf[u, h, dn, :, hi] = (
-                pbuf[u, h, dn, :, hi].astype(F32) + x1[u, h, 1].astype(F32)
-            ).astype(BF16)
-            rs_copy(u, h, 3).start()
-
-    def sum3(u, h, p1, c2):
+        for p in range(2):
+            piece = parts[p]
+            for h in range(2):
+                for way in range(2):
+                    rows = (lo, hi)[way]
+                    side = (up, down)[way]
+                    rs_copy(u, h, 2 * p + way).wait_recv()
+                    pbuf[u, h, side, piece, rows] = (
+                        pbuf[u, h, side, piece, rows].astype(F32) + x1[u, h, way, piece].astype(F32)
+                    ).astype(BF16)
+                    rs_copy(u, h, 4 + 2 * p + way).start()
+
+    def sum3(u, h, c2):
         return (
-            pbuf[u, h, p1, c2].astype(F32) + x2[u, h, 0, c2].astype(F32) + x2[u, h, 1, c2].astype(F32)
+            pbuf[u, h, here, c2].astype(F32) + x2[u, h, 0, c2].astype(F32) + x2[u, h, 1, c2].astype(F32)
         )
 
     def rs3(u):
-        for h in range(2):
-            p1, p2 = rpos(h)
-            rs_copy(u, h, 2).wait_recv()
-            rs_copy(u, h, 3).wait_recv()
-            for k, d in ((6, 2), (4, 1), (5, -1)):
-                c2 = wrap(p2 + d)
-                s2[u, h, c2] = sum3(u, h, p1, c2).astype(BF16)
-                rs_copy(u, h, k).start()
+        for p in range(2):
+            for h in range(2):
+                rs_copy(u, h, 4 + 2 * p).wait_recv()
+                rs_copy(u, h, 5 + 2 * p).wait_recv()
+                for c2 in (ahead, up) if p == 0 else (down,):
+                    s2[u, h, c2] = sum3(u, h, c2).astype(BF16)
+                    rs_copy(u, h, 8 + c2).start()
 
     def rs4(u):
         for h in range(2):
-            p1, p2 = rpos(h)
-            total = sum3(u, h, p1, p2)
+            total = sum3(u, h, here)
             for k in range(3):
-                rs_copy(u, h, 4 + k).wait_recv()
+                rs_copy(u, h, 8 + k).wait_recv()
                 total = total + x3[u, h, k].astype(F32)
             rows = pl.ds(u * half + h * quart, quart)
             hid[rows, :] = (hid[rows, :].astype(F32) + total).astype(BF16)
@@ -345,10 +354,6 @@
         for d in range(1, n_tp):
             ar1(d, True).start()
 
-        @pl.when(l == 0)
-        def _():
-            in_c.wait()
-
         ag_wait(0, 0, 1)
         ag_start(0, 8, 9, 12, 13)
         ag_wait(0, 4, 5)
@@ -358,6 +363,9 @@
 
         @pl.when(l == 0)
         def _():
+            in_c.wait()
+            for c in (first_copies[1], first_copies[3], later_copies[0], later_copies[1], later_copies[3]):
+                c.start()
             regroup(0, nreg // 4)
 
         ag_wait(1, 0, 1)
@@ -569,16 +577,13 @@
                 gate = proj[rs, pl.ds(chans + cb * LANE, LANE)]
                 gated[rs, cs] = (shrunk * (gate / (1.0 + jnp.exp(-gate)))).astype(BF16)
 
-        others = ((0, 0), (0, 1), (0, -1), (1, 0), (-1, 0), (1, 1), (1, -1), (-1, 1), (-1, -1))
         finish(0, 0, ncb)
         out_c.wait()
         rs1(l, 0)
-        omm(l, 0, others)
         finish(1, 0, ncb // 2)
         rs2(0)
         finish(1, ncb // 2, ncb)
         rs1(l, 1)
-        omm(l, 1, others)
 
         @pl.when(l + 1 < layers)
         def _():
@@ -603,7 +608,7 @@
         rs4(1)
         for u in range(2):
             for h in range(2):
-                for k in range(7):
+                for k in range(11):
                     rs_copy(u, h, k).wait_send()
         for q in range(1, n_seq):
             @pl.when(q > seqi)
@@ -685,8 +690,8 @@
             dma((layers, n_seq)),
             dma((layers, n_seq)),
             dma((layers, n_seq)),
-            dma((2, 2, 8)),
-            dma((2, 2, 8)),
+            dma((2, 2, 11)),
+            dma((2, 2, 11)),
         ],
         compiler_params=pltpu.CompilerParams(
             collective_id=0, has_side_effects=True, vmem_limit_bytes=60 * 1024 * 1024

time: 115 us -> 112 us (0.974)
  Pallas kernels: 113 us -> 110 us
    pallas_call x1, Pallas kernels: 113 us -> 110 us  [per_device(): pl.pallas_call(functools.partial(kernel_body, dims), out_shape=jax.ShapeD...]
where the time goes in v3:
time: 112 us
  Pallas kernels  110 us (98%)
  local copies, waits for them, and re-layouts  1.57 us (1%)
    pallas_call x1, Pallas kernels, per_device(): pl.pallas_call(functools.partial(kernel_body, dims), out_shape=jax.ShapeD...  110 us

profile of v3, /device:TPU:6, one launch (start us, length us, event | category | flops | bytes accessed | tf_op | source)
XLA Modules:
  0.0 112.0 jit_solution(12101247385768238758)
XLA Ops:
  0.0 110.4 %shard_map.100 = bf16[256,256]{1,0:T(8,128)(2,1)} custom-call(bf16[256,256]{1,0:T(8,128)(2,1)} %tok_ref.1, f32[2,4096]{1,0:T(2,128)} %gain_ref.1, bf16[2,32768,128]{2,1,0:T(8,128)(2,1)} %bitcast.6, bf16[2,288,256]{2,1,0:T(8,128)(2,1)} %bitcast.7, bf16[2,256,512]{2,1,0:T(8,128)(2,1)} %w_dt_hbm.1, f32[2,16,512]{2,1,0:T(8,128)} %a_ref.1, f32[2,512]{1,0:T(2,128)} %bias_ref.1, ...), custom_call_target="tpu_custom_call" | custom-call | tf_op jit(solution)/shard_map/pallas_call | solution.py:640
  110.4 1.6 %copy.13 = bf16[256,256]{1,0:T(8,128)(2,1)} copy(bf16[256,256]{1,0:T(8,128)(2,1)} %shard_map.100) | data formatting | bytes 262144

commit v4 on v3

v4 whole, which is shorter than its diff:
```python
import functools
import math

import jax
import jax.numpy as jnp
from jax import lax
from jax.experimental import pallas as pl
from jax.experimental.pallas import tpu as pltpu
from jax.sharding import PartitionSpec as P

MESH = pl.DeviceIdType.MESH
F32 = jnp.float32
BF16 = jnp.bfloat16
SUB = 8
LANE = 128
SIDE = 4
LOG2E = math.log2(math.e)
OFFS = (0, -1, 1, 2)
OUT = (2, 1, -1, 0)
WIDE = 8
AG_KEYS = (0, 1, 2) + tuple(range(4, 20))


def kernel_body(
    dims,
    tok_ref,
    gain_ref,
    w_in_hbm,
    w_low_hbm,
    w_dt_hbm,
    a_ref,
    bias_ref,
    skip_ref,
    thresh_ref,
    w_out_hbm,
    out_ref,
    raw,
    seld,
    w_in_v,
    w_low_v,
    w_dt_v,
    w_out_v,
    hid,
    agbuf,
    sqv,
    facv,
    selp,
    arrecv,
    arres,
    expand_b,
    expand_c,
    bx,
    cx,
    step,
    cum,
    proj,
    yv,
    pin,
    ein,
    hdev,
    hrun,
    esend_f,
    esend,
    erecv,
    tsend,
    trecv,
    spread,
    obuf,
    orecv,
    gated,
    pbuf,
    x1,
    x2,
    s2,
    x3,
    wsem,
    ag_s,
    ag_r,
    ar1_s,
    ar1_r,
    ar2_s,
    ar2_r,
    t_s,
    t_r,
    e_s,
    e_r,
    d_s,
    d_r,
    o_s,
    o_r,
    rs_s,
    rs_r,
):
    layers, n_seq, toks, feat, chans, states, rank = dims
    n_tp = SIDE * SIDE
    half = toks // 2
    quart = toks // 4
    eighth = toks // 8
    per_d = 2 * chans // LANE
    steps = toks // SUB
    arow = toks // n_tp
    ncb = chans // LANE
    seqi = lax.axis_index("seq")
    tpi = lax.axis_index("tp")
    zc = tpi // SIDE
    yc = lax.rem(tpi, SIDE)

    def wrap(v):
        return lax.rem(v + 2 * SIDE, SIDE)

    pos = ((yc, zc), (zc, yc))

    def blk(h, c1, c2):
        return c2 * SIDE + c1 if h == 0 else c1 * SIDE + c2

    def nb(h, axis, d):
        p1, p2 = pos[h]
        if axis == 1:
            return {"tp": blk(h, wrap(p1 + d), p2)}
        return {"tp": blk(h, p1, wrap(p2 + d))}

    def rcopy(src, dst, ssem, rsem, dev):
        return pltpu.make_async_remote_copy(
            src_ref=src, dst_ref=dst, send_sem=ssem, recv_sem=rsem,
            device_id=dev, device_id_type=MESH,
        )

    def wcopies(l):
        return (
            pltpu.make_async_copy(w_low_hbm.at[l], w_low_v.at[l, : rank + 2 * states], wsem.at[l, 0]),
            pltpu.make_async_copy(w_dt_hbm.at[l], w_dt_v.at[l], wsem.at[l, 1]),
            pltpu.make_async_copy(w_in_hbm.at[l], raw, wsem.at[l, 2]),
            pltpu.make_async_copy(w_out_hbm.at[l], w_out_v.at[l], wsem.at[l, 3]),
        )

    first_copies = wcopies(0)
    later_copies = wcopies(1)
    for c in (first_copies[0], first_copies[2]):
        c.start()

    barrier = pltpu.get_barrier_semaphore()
    for d in range(1, n_tp):
        pl.semaphore_signal(barrier, inc=1, device_id={"tp": lax.rem(tpi + d, n_tp)}, device_id_type=MESH)
    for d in range(1, n_seq):
        pl.semaphore_signal(barrier, inc=1, device_id={"seq": lax.rem(seqi + d, n_seq)}, device_id_type=MESH)
    pl.semaphore_wait(barrier, n_tp + n_seq - 2)

    hn = n_seq // 2
    seq_half, seq_rest = seqi // hn, lax.rem(seqi, hn)

    def spread_copy(b, q):
        return rcopy(
            tok_ref.at[pl.ds(b * half, half)], spread.at[seq_half], d_s.at[b], d_r.at[seq_half], {"seq": q}
        )

    def spread_wait(u):
        src = u * hn + seqi // 2

        @pl.when(src != seqi)
        def _():
            rcopy(
                tok_ref.at[pl.ds(0, half)], spread.at[u], d_s.at[0], d_r.at[u], {"seq": src}
            ).wait_recv()

    for b in range(2):
        q = 2 * seq_rest + b

        @pl.when(q != seqi)
        def _():
            spread_copy(b, q).start()

        @pl.when(q == seqi)
        def _():
            spread[seq_half] = tok_ref[b * half : (b + 1) * half, :]

    hsteps = steps // 2
    ri = lax.broadcasted_iota(jnp.int32, (half, half), 0)
    ci = lax.broadcasted_iota(jnp.int32, (half, half), 1)
    perm = jnp.where(ci == lax.rem(ri, SUB) * hsteps + ri // SUB, 1.0, 0.0).astype(BF16)

    def ag_info(u, h, k):
        p1, p2 = pos[h]
        r0 = u * half + h * quart
        full = pl.ds(r0, quart)
        lo = pl.ds(r0, eighth)
        hi = pl.ds(r0 + eighth, eighth)
        if k < 4:
            to = (1, -1, 2)[k]
            src_d, dst_d, rows, ax = 0, -to, full, 1

            def at(d):
                return blk(h, wrap(p1 + d), p2)
        else:
            src_d, dst_d, rows, to = (
                (0, -1, full, 1),
                (0, 1, full, -1),
                (-1, -2, lo, 1),
                (1, 2, hi, -1),
            )[(k - 4) % 4]
            o = OFFS[(k - 4) // 4]
            ax = 2

            def at(d):
                return blk(h, wrap(p1 + o), wrap(p2 + d))

        return at(src_d), at(dst_d), rows, nb(h, ax, to)

    def ag_send(u, h, k):
        src, _, rows, dev = ag_info(u, h, k)
        ref = agbuf.at[src, rows]
        return rcopy(ref, ref, ag_s.at[u, h, k], ag_r.at[u, h, k], dev)

    def ag_start(u, *ks):
        for k in ks:
            for h in range(2):
                ag_send(u, h, k).start()

    def ag_wait(u, *ks):
        for k in ks:
            for h in range(2):
                _, dst, rows, dev = ag_info(u, h, k)
                ref = agbuf.at[dst, rows]
                rcopy(ref, ref, ag_s.at[u, h, k], ag_r.at[u, h, k], dev).wait_recv()

    def publish(l, u):
        rows = pl.ds(u * half, half)
        own = hid[rows, :].astype(F32)
        gain_row = gain_ref[pl.ds(l, 1), pl.ds(pl.multiple_of(tpi * feat, feat), feat)]
        agbuf[tpi, rows] = (own * gain_row).astype(BF16)
        sqv[rows, :] = jnp.broadcast_to(jnp.sum(own * own, axis=1, keepdims=True), (half, LANE))
        ag_start(u, 0, 1, 4, 5, 2)


    ei = lax.broadcasted_iota(jnp.int32, (LANE, states * LANE), 0)
    ej = lax.broadcasted_iota(jnp.int32, (LANE, states * LANE), 1) // LANE
    expand_b[...] = jnp.where(ei == ej, 1.0, 0.0).astype(BF16)
    expand_c[...] = jnp.where(ei == ej + states, 1.0, 0.0).astype(BF16)
    grp = 2 * LANE // per_d
    gi = lax.broadcasted_iota(jnp.int32, (2 * LANE, 2 * LANE), 0)
    gj = lax.broadcasted_iota(jnp.int32, (2 * LANE, 2 * LANE), 1)
    seld[...] = jnp.where(gj == lax.rem(gi, grp) * per_d + gi // grp, 1.0, 0.0).astype(BF16)
    sel_w = rank + LANE
    pad_from = rank + 2 * states
    for l in range(layers):
        w_low_v[l, pad_from:, :] = jnp.zeros((sel_w - pad_from, feat), BF16)

    def regroup(b0, b1):
        def one(i, unused):
            r = pl.multiple_of(i * WIDE * 2 * LANE, WIDE * 2 * LANE)
            parts = [raw[pl.ds(r + v * 2 * LANE, 2 * LANE), :] for v in range(WIDE)]
            got = jnp.dot(
                seld[...], jnp.concatenate(parts, axis=1), preferred_element_type=F32
            ).astype(BF16)
            d0 = pl.multiple_of(i * WIDE * grp, WIDE * grp)
            for q in range(per_d):
                cols = pl.ds((q % 2) * chans + (q // 2) * LANE, LANE)
                for v in range(WIDE):
                    w_in_v[pl.ds(d0 + v * grp, grp), cols] = got[
                        q * grp : (q + 1) * grp, v * LANE : (v + 1) * LANE
                    ]
            return unused

        lax.fori_loop(b0, b1, one, 0)

    nreg = n_tp * feat // (WIDE * grp)

    def seq_copy(l, u, src, dst, ss, rs, q, sending):
        slot = seqi if sending else q
        return rcopy(
            src.at[l, u], dst.at[l, u, slot], ss.at[l, u, q], rs.at[l, u, slot], {"seq": q}
        )

    def t_copy(l, u, q, sending):
        return seq_copy(l, u, tsend, trecv, t_s, t_r, q, sending)

    def e_copy(l, u, q, sending):
        return seq_copy(l, u, esend, erecv, e_s, e_r, q, sending)

    def to_peers(u, act):
        for q in range(n_seq):
            @pl.when((q != seqi) if u == 0 else (q > seqi))
            def _():
                act(q)

    lo = pl.ds(0, eighth)
    hi = pl.ds(eighth, eighth)

    def rpos(h):
        p2, p1 = pos[h]
        return p1, p2

    def rnb(h, axis, d):
        return nb(h, 3 - axis, d)

    ahead, up, down, here = range(SIDE)
    parts = (pl.ds(0, 2), pl.ds(2, 2))

    def rs_copy(u, h, k):
        if k < 8:
            piece = parts[(k // 2) % 2]
            way = k % 2
            if k < 4:
                src = pbuf.at[u, h, ahead, piece, (lo, hi)[way]]
                dst = x1.at[u, h, way, piece]
            else:
                src = pbuf.at[u, h, (up, down)[way], piece]
                dst = x2.at[u, h, way, piece]
            dev = rnb(h, 1, (1, -1)[way])
        else:
            src = s2.at[u, h, (ahead, up, down)[k - 8]]
            dst = x3.at[u, h, k - 8]
            dev = rnb(h, 2, OUT[k - 8])
        return rcopy(src, dst, rs_s.at[u, h, k], rs_r.at[u, h, k], dev)

    def omm(l, u, pairs):
        lhs = gated[u * half : (u + 1) * half, :]
        for dz, dy in pairs:
            z, y = wrap(zc + dz), wrap(yc + dy)
            cols = pl.ds(pl.multiple_of((z * SIDE + y) * feat, feat), feat)
            val = jnp.dot(lhs, w_out_v[l, :, cols], preferred_element_type=F32).astype(BF16)
            iz, iy = OUT.index(dz), OUT.index(dy)
            pbuf[u, 0, iz, iy] = val[:quart]
            pbuf[u, 1, iy, iz] = val[quart:]

    def rs1(l, u):
        omm(l, u, ((2, 2), (2, 1), (1, 2)))
        for h in range(2):
            rs_copy(u, h, 0).start()
            rs_copy(u, h, 1).start()
        omm(l, u, ((2, -1), (2, 0), (-1, 2), (0, 2)))
        for h in range(2):
            rs_copy(u, h, 2).start()
            rs_copy(u, h, 3).start()
        omm(l, u, ((1, 1), (1, -1), (1, 0), (-1, 1), (-1, -1), (-1, 0), (0, 1), (0, -1)))
        omm(l, u, ((0, 0),))

    def rs2(u):
        for p in range(2):
            piece = parts[p]
            for h in range(2):
                for way in range(2):
                    rows = (lo, hi)[way]
                    side = (up, down)[way]
                    rs_copy(u, h, 2 * p + way).wait_recv()
                    pbuf[u, h, side, piece, rows] = (
                        pbuf[u, h, side, piece, rows].astype(F32) + x1[u, h, way, piece].astype(F32)
                    ).astype(BF16)
                    rs_copy(u, h, 4 + 2 * p + way).start()

    def sum3(u, h, c2):
        return (
            pbuf[u, h, here, c2].astype(F32) + x2[u, h, 0, c2].astype(F32) + x2[u, h, 1, c2].astype(F32)
        )

    def rs3(u):
        for p in range(2):
            for h in range(2):
                rs_copy(u, h, 4 + 2 * p).wait_recv()
                rs_copy(u, h, 5 + 2 * p).wait_recv()
                for c2 in (ahead, up) if p == 0 else (down,):
                    s2[u, h, c2] = sum3(u, h, c2).astype(BF16)
                    rs_copy(u, h, 8 + c2).start()

    def rs4(u):
        for h in range(2):
            total = sum3(u, h, here)
            for k in range(3):
                rs_copy(u, h, 8 + k).wait_recv()
                total = total + x3[u, h, k].astype(F32)
            rows = pl.ds(u * half + h * quart, quart)
            hid[rows, :] = (hid[rows, :].astype(F32) + total).astype(BF16)

    hred = n_tp // 2

    def sel_copy(u, d, sending):
        to = u * hred + lax.rem(tpi + d, hred)
        rows = pl.ds(pl.multiple_of(u * half + lax.rem(tpi + d, hred) * arow, arow), arow)
        return rcopy(selp.at[rows], arrecv.at[tpi], ar1_s.at[u, d], ar1_r.at[tpi], {"tp": to})

    def each_reducer(u, act):
        for d in range(hred):
            if d == 0:
                @pl.when(tpi // hred != u)
                def _():
                    act(0)
            else:
                act(d)

    def sel(l, u):
        rs = pl.ds(u * half, half)
        selv = lax.dot_general(
            agbuf[tpi, rs], w_low_v[l], (((1,), (1,)), ((), ())), preferred_element_type=F32
        )
        sq = sqv[rs, 0:1]
        sq_hi = sq.astype(BF16).astype(F32)
        lane = lax.broadcasted_iota(jnp.int32, (half, sel_w), 1)
        selv = jnp.where(lane == pad_from, sq_hi, selv)
        selv = jnp.where(lane == pad_from + 1, sq - sq_hi, selv)
        selp[rs, :] = selv.astype(BF16)
        each_reducer(u, lambda d: sel_copy(u, d, True).start())

        @pl.when(tpi // hred == u)
        def _():
            own = pl.ds(pl.multiple_of(u * half + lax.rem(tpi, hred) * arow, arow), arow)
            arrecv[tpi] = selp[own, :]

    def res_copy(u, d):
        rows = pl.ds(pl.multiple_of(u * half + lax.rem(tpi, hred) * arow, arow), arow)
        return rcopy(
            arres.at[rows], arres.at[rows], ar2_s.at[d], ar2_r.at[u, lax.rem(tpi, hred)],
            {"tp": lax.rem(tpi + d, n_tp)},
        )

    def res_wait(u, d):
        i = lax.rem(tpi + d, hred)
        rows = pl.ds(pl.multiple_of(u * half + i * arow, arow), arow)
        rcopy(
            arres.at[rows], arres.at[rows], ar2_s.at[0], ar2_r.at[u, i], {"tp": u * hred + i}
        ).wait_recv()

    def red(u):
        @pl.when(tpi // hred == u)
        def _():
            for d in range(1, n_tp):
                fr = lax.rem(tpi + n_tp - d, n_tp)
                rcopy(
                    selp.at[pl.ds(0, arow)], arrecv.at[fr], ar1_s.at[u, 0], ar1_r.at[fr], {"tp": fr}
                ).wait_recv()
            tot = jnp.zeros((arow, sel_w), F32)
            for i in range(n_tp):
                tot = tot + arrecv[i].astype(F32)
            lane = lax.broadcasted_iota(jnp.int32, (arow, sel_w), 1)
            is_sq = (lane == pad_from) | (lane == pad_from + 1)
            ssum = jnp.sum(jnp.where(is_sq, tot, 0.0), axis=1, keepdims=True)
            factor = lax.rsqrt(ssum / (n_tp * feat) + 1e-05)
            f_hi = factor.astype(BF16).astype(F32)
            tot = jnp.where(
                lane == pad_from, f_hi, jnp.where(lane == pad_from + 1, factor - f_hi, tot * factor)
            )
            mine = pl.ds(pl.multiple_of(u * half + lax.rem(tpi, hred) * arow, arow), arow)
            arres[mine, :] = tot.astype(BF16)
            for d in range(1, n_tp):
                res_copy(u, d).start()

    def dt(l, u):
        rs = pl.ds(u * half, half)
        each_reducer(u, lambda d: res_wait(u, d))
        tail = arres[rs, rank:]
        tl = lax.broadcasted_iota(jnp.int32, (half, LANE), 1)
        in_f = (tl == 2 * states) | (tl == 2 * states + 1)
        fac = jnp.sum(jnp.where(in_f, tail.astype(F32), 0.0), axis=1, keepdims=True)
        facv[rs, :] = jnp.broadcast_to(fac, (half, LANE))
        pre = jnp.dot(arres[rs, :rank], w_dt_v[l], preferred_element_type=F32) + bias_ref[pl.ds(l, 1), :]
        step[rs, :] = jnp.maximum(pre, 0.0) + jnp.log1p(jnp.exp(-jnp.abs(pre)))
        bx[rs, :] = jnp.dot(tail, expand_b[...], preferred_element_type=F32)
        cx[rs, :] = jnp.dot(tail, expand_c[...], preferred_element_type=F32)

        def accum(t, run):
            rows = pl.ds(pl.multiple_of(t * SUB, SUB), SUB)
            run = run + step[rows, :]
            cum[rows, :] = run
            return run

        ctot = lax.fori_loop(u * hsteps, (u + 1) * hsteps, accum, jnp.zeros((SUB, chans), F32))
        both = jnp.broadcast_to(jnp.sum(ctot, axis=0, keepdims=True), (SUB, chans))
        tsend[l, u] = both
        trecv[l, u, seqi] = both
        to_peers(u, lambda q: t_copy(l, u, q, True).start())

    def ag_g2(u):
        ag_wait(u, 0, 1)
        ag_start(u, 8, 9, 12, 13)
        ag_wait(u, 4, 5)
        ag_start(u, 6, 7)
        ag_wait(u, 2)
        ag_start(u, 16, 17)

    def ag_g3(u):
        ag_wait(u, 8, 9)
        ag_start(u, 10, 11)
        ag_wait(u, 12, 13)
        ag_start(u, 14, 15)
        ag_wait(u, 16, 17)
        ag_start(u, 18, 19)

    near = ((0, 0), (0, 1), (0, -1), (1, 0), (-1, 0), (1, 1), (1, -1), (-1, 1), (-1, -1))
    away = ((2, 0), (2, 1), (2, 2), (2, 3), (0, 2), (1, 2), (3, 2))

    def mm(u, first, pairs):
        rs = pl.ds(u * half, half)
        for i, (dz, dy) in enumerate(pairs):
            b = wrap(zc + dz) * SIDE + wrap(yc + dy)
            rows = pl.ds(pl.multiple_of(b * feat, feat), feat)
            val = jnp.dot(agbuf[b, rs], w_in_v[rows, :], preferred_element_type=F32)
            if first and i == 0:
                proj[rs, :] = val
            else:
                proj[rs, :] += val

    def project(u):
        mm(u, True, near)
        ag_wait(u, 6, 7, 10, 11, 14, 15, 18, 19)
        mm(u, False, away)
        rs = pl.ds(u * half, half)
        proj[rs, :] = proj[rs, :] * facv[rs, 0:1]

    def decay_rows(l, cs):
        return [
            jnp.broadcast_to(a_ref[l, s : s + 1, cs] * (-LOG2E), (SUB, LANE)) for s in range(states)
        ]

    def scan(l, u):
        skip_row = skip_ref[pl.ds(l, 1), :]
        for cb in range(ncb):
            cs = pl.ds(cb * LANE, LANE)
            na = decay_rows(l, cs)
            skip = skip_row[:, cb * LANE : (cb + 1) * LANE]

            def scan_step(t, hs):
                rows = pl.ds(pl.multiple_of(t * SUB, SUB), SUB)
                st = step[rows, cs]
                cur = proj[rows, cs]
                dr = st * cur
                acc = skip * cur
                new = []
                for s in range(states):
                    ls = pl.ds(s * LANE, LANE)
                    hn = jnp.exp2(st * na[s]) * hs[s] + bx[rows, ls] * dr
                    acc = acc + cx[rows, ls] * hn
                    new.append(hn)
                yv[rows, cs] = acc
                return tuple(new)

            init = tuple(jnp.zeros((SUB, LANE), F32) for _ in range(states))
            hs = lax.fori_loop(u * hsteps, (u + 1) * hsteps, scan_step, init, unroll=2)
            sub = lax.broadcasted_iota(jnp.int32, (SUB, LANE), 0)
            ct = cum[pl.ds(((u + 1) * hsteps - 1) * SUB, SUB), cs]
            for s in range(states):
                e = hs[s]
                p = jnp.exp2(ct * na[s])
                for d in (1, 2, 4):
                    ok = sub >= d
                    e = e + jnp.where(ok, p * pltpu.roll(e, d, 0), 0.0)
                    p = p * jnp.where(ok, pltpu.roll(p, d, 0), 1.0)
                esend_f[s : s + 1, cs] = e[SUB - 1 : SUB, :]
                ein[s, :, cs] = jnp.where(sub >= 1, pltpu.roll(e, 1, 0), 0.0)
                pin[s, :, cs] = jnp.where(sub >= 1, pltpu.roll(p, 1, 0), 1.0)
        ends = esend_f[...].astype(BF16)
        esend[l, u] = ends
        erecv[l, u, seqi] = ends
        to_peers(u, lambda q: e_copy(l, u, q, True).start())

    def absorb(l, u, q):
        dec = jnp.exp2(a_ref[l] * (-LOG2E) * trecv[l, u, q, 0:1, :])
        hrun[...] = dec * hrun[...] + erecv[l, u, q].astype(F32)

    def arrive(l, u, q):
        t_copy(l, u, q, False).wait_recv()
        e_copy(l, u, q, False).wait_recv()

    def carry(l, u):
        if u == 0:
            hrun[...] = jnp.zeros_like(hrun)
        else:
            for q in range(n_seq):
                @pl.when(q > seqi)
                def _():
                    arrive(l, 0, q)

                @pl.when(q >= seqi)
                def _():
                    absorb(l, 0, q)
        for q in range(n_seq - 1):
            @pl.when(q < seqi)
            def _():
                arrive(l, u, q)
                absorb(l, u, q)
        hdev[...] = hrun[...]

    def finish(l, u, c0, c1):
        rs = pl.ds(u * half, half)
        th_row = thresh_ref[pl.ds(l, 1), :]
        for cb in range(c0, c1):
            cs = pl.ds(cb * LANE, LANE)
            na = decay_rows(l, cs)
            hin = [ein[s, :, cs] + pin[s, :, cs] * hdev[s : s + 1, cs] for s in range(states)]
            th = th_row[:, cb * LANE : (cb + 1) * LANE]

            def fold(t, unused):
                rows = pl.ds(pl.multiple_of(t * SUB, SUB), SUB)
                ct = cum[rows, cs]
                acc = yv[rows, cs]
                for s in range(states):
                    ls = pl.ds(s * LANE, LANE)
                    acc = acc + cx[rows, ls] * (jnp.exp2(ct * na[s]) * hin[s])
                yv[rows, cs] = acc
                return unused

            lax.fori_loop(u * hsteps, (u + 1) * hsteps, fold, 0, unroll=4)

            mixed = yv[rs, cs]
            fct = lax.rsqrt(jnp.mean(mixed * mixed, axis=1, keepdims=True) + 1e-05)
            normal = mixed * fct
            shrunk = jnp.maximum(normal - th, 0.0) - jnp.maximum(-normal - th, 0.0)
            gate = proj[rs, pl.ds(chans + cb * LANE, LANE)]
            gated[rs, cs] = (shrunk * (gate / (1.0 + jnp.exp(-gate)))).astype(BF16)

    def gather_sent(u):
        for h in range(2):
            for k in AG_KEYS:
                ag_send(u, h, k).wait_send()

    def sent(u):
        for h in range(2):
            for k in range(11):
                rs_copy(u, h, k).wait_send()
        each_reducer(u, lambda d: sel_copy(u, d, True).wait_send())

        @pl.when(tpi // hred == u)
        def _():
            for d in range(1, n_tp):
                res_copy(u, d).wait_send()

    low_c, in_c, dt_c, out_c = first_copies[0], first_copies[2], first_copies[1], first_copies[3]
    for u in range(2):
        spread_wait(u)
        rs = pl.ds(u * half, half)
        hid[rs, :] = jnp.dot(perm, spread[u], preferred_element_type=F32).astype(BF16)
        publish(0, u)
        if u == 0:
            low_c.wait()
        sel(0, u)
    ag_g2(0)
    in_c.wait()
    for c in (dt_c, out_c, later_copies[0], later_copies[1], later_copies[3]):
        c.start()
    regroup(0, nreg // 2)
    ag_g3(0)
    red(0)
    regroup(nreg // 2, nreg)
    later_copies[2].start()
    dt_c.wait()
    dt(0, 0)

    def layer(l, unused):
        more = l + 1 < layers
        project(0)
        ag_g2(1)
        scan(l, 0)
        red(1)
        carry(l, 0)
        ag_g3(1)
        finish(l, 0, 0, ncb)

        @pl.when(l == 0)
        def _():
            out_c.wait()

        gather_sent(0)
        rs1(l, 0)
        dt(l, 1)
        rs2(0)
        project(1)
        scan(l, 1)
        rs3(0)
        carry(l, 1)
        finish(l, 1, 0, ncb // 2)
        rs4(0)
        sent(0)

        @pl.when(more)
        def _():
            for i in (0, 1, 3):
                later_copies[i].wait()
            publish(l + 1, 0)
            sel(l + 1, 0)

        finish(l, 1, ncb // 2, ncb)
        gather_sent(1)
        rs1(l, 1)

        @pl.when(more)
        def _():
            later_copies[2].wait()
            regroup(0, nreg // 2)
            ag_g2(0)

        rs2(1)

        @pl.when(more)
        def _():
            regroup(nreg // 2, nreg)
            red(0)
            ag_g3(0)

        rs3(1)

        @pl.when(more)
        def _():
            dt(l + 1, 0)

        rs4(1)
        sent(1)

        @pl.when(more)
        def _():
            publish(l + 1, 1)
            sel(l + 1, 1)

        for u in range(2):
            to_peers(u, lambda q: t_copy(l, u, q, True).wait_send())
            to_peers(u, lambda q: e_copy(l, u, q, True).wait_send())
        return unused

    lax.fori_loop(0, layers, layer, 0)

    for b in range(2):
        q = 2 * seq_rest + b

        @pl.when(q != seqi)
        def _():
            spread_copy(b, q).wait_send()

    odd = lax.rem(seqi, 2)
    for u in range(2):
        obuf[u] = lax.dot_general(
            perm, hid[u * half : (u + 1) * half, :], (((0,), (0,)), ((), ())), preferred_element_type=F32
        ).astype(BF16)
        dst = u * hn + seqi // 2

        @pl.when(dst != seqi)
        def _():
            rcopy(obuf.at[u], orecv.at[odd], o_s.at[u], o_r.at[odd], {"seq": dst}).start()

        @pl.when(dst == seqi)
        def _():
            orecv[odd] = obuf[u]

    for b in range(2):
        src = 2 * seq_rest + b

        @pl.when(src != seqi)
        def _():
            rcopy(obuf.at[0], orecv.at[b], o_s.at[0], o_r.at[b], {"seq": src}).wait_recv()

        out_ref[b * half : (b + 1) * half, :] = orecv[b]
    for u in range(2):
        dst = u * hn + seqi // 2

        @pl.when(dst != seqi)
        def _():
            rcopy(obuf.at[u], orecv.at[odd], o_s.at[u], o_r.at[odd], {"seq": dst}).wait_send()


def per_device(n_seq, tokens, norm_gain, w_in, w_low, w_dt, a_rate, dt_bias, skip_gain, threshold, w_out):
    toks, feat = tokens.shape
    layers, model, _, chans = w_in.shape
    states = a_rate.shape[1]
    rank = w_dt.shape[1]
    n_tp = SIDE * SIDE
    half, quart, eighth = toks // 2, toks // 4, toks // 8
    per_d = 2 * chans // LANE
    sel_w = rank + LANE
    dims = (layers, n_seq, toks, feat, chans, states, rank)
    vm = pl.BlockSpec(memory_space=pltpu.VMEM)
    hb = pl.BlockSpec(memory_space=pl.ANY)
    dma = pltpu.SemaphoreType.DMA
    V = pltpu.VMEM
    return pl.pallas_call(
        functools.partial(kernel_body, dims),
        out_shape=jax.ShapeDtypeStruct((toks, feat), BF16),
        in_specs=[vm, vm, hb, hb, hb, vm, vm, vm, vm, hb],
        out_specs=vm,
        scratch_shapes=[
            V((model * per_d, LANE), BF16),
            V((2 * LANE, 2 * LANE), BF16),
            V((model, 2 * chans), BF16),
            V((layers, sel_w, feat), BF16),
            V((layers, rank, chans), BF16),
            V((layers, chans, model), BF16),
            V((toks, feat), BF16),
            V((n_tp, toks, feat), BF16),
            V((toks, LANE), F32),
            V((toks, LANE), F32),
            V((toks, sel_w), BF16),
            V((n_tp, toks // n_tp, sel_w), BF16),
            V((toks, sel_w), BF16),
            V((LANE, states * LANE), BF16),
            V((LANE, states * LANE), BF16),
            V((toks, states * LANE), F32),
            V((toks, states * LANE), F32),
            V((toks, chans), F32),
            V((toks, chans), F32),
            V((toks, 2 * chans), F32),
            V((toks, chans), F32),
            V((states, SUB, chans), F32),
            V((states, SUB, chans), F32),
            V((states, chans), F32),
            V((states, chans), F32),
            V((states, chans), F32),
            V((layers, 2, states, chans), BF16),
            V((layers, 2, n_seq, states, chans), BF16),
            V((layers, 2, SUB, chans), F32),
            V((layers, 2, n_seq, SUB, chans), F32),
            V((2, half, feat), BF16),
            V((2, half, feat), BF16),
            V((2, half, feat), BF16),
            V((toks, chans), BF16),
            V((2, 2, SIDE, SIDE, quart, feat), BF16),
            V((2, 2, 2, SIDE, eighth, feat), BF16),
            V((2, 2, 2, SIDE, quart, feat), BF16),
            V((2, 2, SIDE, quart, feat), BF16),
            V((2, 2, 3, quart, feat), BF16),
            dma((layers, 4)),
            dma((2, 2, 20)),
            dma((2, 2, 20)),
            dma((2, n_tp // 2)),
            dma((n_tp,)),
            dma((n_tp,)),
            dma((2, n_tp // 2)),
            dma((layers, 2, n_seq)),
            dma((layers, 2, n_seq)),
            dma((layers, 2, n_seq)),
            dma((layers, 2, n_seq)),
            dma((2,)),
            dma((2,)),
            dma((2,)),
            dma((2,)),
            dma((2, 2, 11)),
            dma((2, 2, 11)),
        ],
        compiler_params=pltpu.CompilerParams(
            collective_id=0, has_side_effects=True, vmem_limit_bytes=60 * 1024 * 1024
        ),
    )(
        tokens,
        norm_gain,
        jnp.swapaxes(w_in.reshape(layers, model, 2, chans // LANE, LANE), 2, 3).reshape(
            layers, model * per_d, LANE
        ),
        jnp.swapaxes(w_low, 1, 2),
        w_dt,
        a_rate,
        dt_bias,
        skip_gain,
        threshold,
        w_out,
    )


def solution(mesh):
    in_specs = (
        P("seq", "tp"),
        P(),
        P(None, None, None, "tp"),
        P(None, "tp", None),
        P(None, None, "tp"),
        P(None, None, "tp"),
        P(None, "tp"),
        P(None, "tp"),
        P(None, "tp"),
        P(None, "tp", None),
    )
    return jax.shard_map(
        functools.partial(per_device, mesh.shape["seq"]),
        mesh=mesh,
        in_specs=in_specs,
        out_specs=P("seq", "tp"),
        check_vma=False,
    )
```

time: 112 us -> 117 us (1.045)
  the two profiles are of different devices: /device:TPU:6 before, /device:TPU:3 now
where the time goes in v4:
time: 117 us
  Pallas kernels  115 us (98%)
  local copies, waits for them, and re-layouts  1.57 us (1%)
    pallas_call x1, Pallas kernels, per_device(): pl.pallas_call(functools.partial(kernel_body, dims), out_shape=jax.ShapeD...  115 us

profile of v4, /device:TPU:3, one launch (start us, length us, event | category | flops | bytes accessed | tf_op | source)
XLA Modules:
  0.0 117.0 jit_solution(10974699238685617032)
XLA Ops:
  0.0 115.4 %shard_map.100 = bf16[256,256]{1,0:T(8,128)(2,1)} custom-call(bf16[256,256]{1,0:T(8,128)(2,1)} %tok_ref.1, f32[2,4096]{1,0:T(2,128)} %gain_ref.1, bf16[2,32768,128]{2,1,0:T(8,128)(2,1)} %bitcast.6, bf16[2,288,256]{2,1,0:T(8,128)(2,1)} %bitcast.7, bf16[2,256,512]{2,1,0:T(8,128)(2,1)} %w_dt_hbm.1, f32[2,16,512]{2,1,0:T(8,128)} %a_ref.1, f32[2,512]{1,0:T(2,128)} %bias_ref.1, ...), custom_call_target="tpu_custom_call" | custom-call | tf_op jit(solution)/shard_map/pallas_call | solution.py:769
  115.4 1.6 %copy.13 = bf16[256,256]{1,0:T(8,128)(2,1)} copy(bf16[256,256]{1,0:T(8,128)(2,1)} %shard_map.100) | data formatting | bytes 262144

commit v5 on v3

--- a/solution.py
+++ b/solution.py
@@ -210,7 +210,7 @@
     for l in range(layers):
         w_low_v[l, pad_from:, :] = jnp.zeros((sel_w - pad_from, feat), BF16)
 
-    def regroup(b0, b1):
+    def regroup(l, b0, b1):
         def one(i, unused):
             r = pl.multiple_of(i * WIDE * 2 * LANE, WIDE * 2 * LANE)
             parts = [raw[pl.ds(r + v * 2 * LANE, 2 * LANE), :] for v in range(WIDE)]
@@ -221,7 +221,7 @@
             for q in range(per_d):
                 cols = pl.ds((q % 2) * chans + (q // 2) * LANE, LANE)
                 for v in range(WIDE):
-                    w_in_v[pl.ds(d0 + v * grp, grp), cols] = got[
+                    w_in_v[l, pl.ds(d0 + v * grp, grp), cols] = got[
                         q * grp : (q + 1) * grp, v * LANE : (v + 1) * LANE
                     ]
             return unused
@@ -366,7 +366,7 @@
             in_c.wait()
             for c in (first_copies[1], first_copies[3], later_copies[0], later_copies[1], later_copies[3]):
                 c.start()
-            regroup(0, nreg // 4)
+            regroup(0, 0, nreg // 4)
 
         ag_wait(1, 0, 1)
         ag_start(1, 8, 9, 12, 13)
@@ -407,7 +407,7 @@
 
         @pl.when(l == 0)
         def _():
-            regroup(nreg // 4, nreg // 2)
+            regroup(0, nreg // 4, nreg // 2)
 
         ag_wait(1, 8, 9)
         ag_start(1, 10, 11)
@@ -418,7 +418,7 @@
 
         @pl.when(l == 0)
         def _():
-            regroup(nreg // 2, nreg)
+            regroup(0, nreg // 2, nreg)
             later_copies[2].start()
 
         for d in range(1, n_tp):
@@ -454,7 +454,7 @@
             for i, (dz, dy) in enumerate(pairs):
                 b = wrap(zc + dz) * SIDE + wrap(yc + dy)
                 rows = pl.ds(pl.multiple_of(b * feat, feat), feat)
-                val = jnp.dot(agbuf[b, rs], w_in_v[rows, :], preferred_element_type=F32)
+                val = jnp.dot(agbuf[b, rs], w_in_v[l, rows, :], preferred_element_type=F32)
                 if first and i == 0:
                     proj[rs, :] = val
                 else:
@@ -491,7 +491,7 @@
                     init = tuple(jnp.zeros((SUB, LANE), F32) for _ in range(states))
                 else:
                     init = tuple(hst[s, :, cs] for s in range(states))
-                hs = lax.fori_loop(u * steps // 2, (u + 1) * steps // 2, scan_step, init, unroll=2)
+                hs = lax.fori_loop(u * steps // 2, (u + 1) * steps // 2, scan_step, init, unroll=4)
                 if u == 0:
                     for s in range(states):
                         hst[s, :, cs] = hs[s]
@@ -509,6 +509,11 @@
                     ein[s, :, cs] = jnp.where(sub >= 1, pltpu.roll(e, 1, 0), 0.0)
                     pin[s, :, cs] = jnp.where(sub >= 1, pltpu.roll(p, 1, 0), 1.0)
 
+        @pl.when(l == 0)
+        def _():
+            later_copies[2].wait()
+            regroup(1, 0, nreg)
+
         ag_wait(0, 6, 7, 10, 11, 14, 15, 18, 19)
         mm(0, True, near + away)
         proj[:half, :] = proj[:half, :] * fac[:half]
@@ -585,24 +590,14 @@
         finish(1, ncb // 2, ncb)
         rs1(l, 1)
 
-        @pl.when(l + 1 < layers)
-        def _():
-            later_copies[2].wait()
-            regroup(0, nreg // 4)
-
         rs2(1)
         rs3(0)
-
-        @pl.when(l + 1 < layers)
-        def _():
-            regroup(nreg // 4, nreg // 2)
 
         rs4(0)
 
         @pl.when(l + 1 < layers)
         def _():
             publish(l + 1, 0)
-            regroup(nreg // 2, nreg)
 
         rs3(1)
         rs4(1)
@@ -645,7 +640,7 @@
         scratch_shapes=[
             V((model * per_d, LANE), BF16),
             V((2 * LANE, 2 * LANE), BF16),
-            V((model, 2 * chans), BF16),
+            V((layers, model, 2 * chans), BF16),
             V((layers, sel_w, feat), BF16),
             V((layers, rank, chans), BF16),
             V((layers, chans, model), BF16),

time: 112 us -> 116 us (1.036)
  Pallas kernels: 110 us -> 114 us
    pallas_call x1, Pallas kernels: 110 us -> 114 us  [per_device(): pl.pallas_call(functools.partial(kernel_body, dims), out_shape=jax.ShapeD...]
where the time goes in v5:
time: 116 us
  Pallas kernels  114 us (98%)
  local copies, waits for them, and re-layouts  1.57 us (1%)
    pallas_call x1, Pallas kernels, per_device(): pl.pallas_call(functools.partial(kernel_body, dims), out_shape=jax.ShapeD...  114 us

profile of v5, /device:TPU:6, one launch (start us, length us, event | category | flops | bytes accessed | tf_op | source)
XLA Modules:
  0.0 115.9 jit_solution(14975460194394542869)
XLA Ops:
  0.0 114.3 %shard_map.100 = bf16[256,256]{1,0:T(8,128)(2,1)} custom-call(bf16[256,256]{1,0:T(8,128)(2,1)} %tok_ref.1, f32[2,4096]{1,0:T(2,128)} %gain_ref.1, bf16[2,32768,128]{2,1,0:T(8,128)(2,1)} %bitcast.6, bf16[2,288,256]{2,1,0:T(8,128)(2,1)} %bitcast.7, bf16[2,256,512]{2,1,0:T(8,128)(2,1)} %w_dt_hbm.1, f32[2,16,512]{2,1,0:T(8,128)} %a_ref.1, f32[2,512]{1,0:T(2,128)} %bias_ref.1, ...), custom_call_target="tpu_custom_call" | custom-call | tf_op jit(solution)/shard_map/pallas_call | solution.py:635
  114.3 1.6 %copy.13 = bf16[256,256]{1,0:T(8,128)(2,1)} copy(bf16[256,256]{1,0:T(8,128)(2,1)} %shard_map.100) | data formatting | bytes 262144

commit v6 on v3

--- a/solution.py
+++ b/solution.py
@@ -421,6 +421,24 @@
             regroup(nreg // 2, nreg)
             later_copies[2].start()
 
+        def mm(u, first, pairs):
+            rs = pl.ds(u * half, half)
+            for i, (dz, dy) in enumerate(pairs):
+                b = wrap(zc + dz) * SIDE + wrap(yc + dy)
+                rows = pl.ds(pl.multiple_of(b * feat, feat), feat)
+                val = jnp.dot(agbuf[b, rs], w_in_v[rows, :], preferred_element_type=F32)
+                if first and i == 0:
+                    proj[rs, :] = val
+                else:
+                    proj[rs, :] += val
+
+        near = ((0, 0), (0, 1), (0, -1), (1, 0), (-1, 0), (1, 1), (1, -1), (-1, 1), (-1, -1))
+        away = ((2, 0), (2, 1), (2, 2), (2, 3), (0, 2), (1, 2), (3, 2))
+
+        mm(0, True, near)
+        ag_wait(0, 6, 7, 10, 11, 14, 15, 18, 19)
+        mm(0, False, away)
+        mm(1, True, near)
         for d in range(1, n_tp):
             ar2(d, False).wait_recv()
         tail = arres[:, rank:]
@@ -448,20 +466,6 @@
 
         skip_row = skip_ref[pl.ds(l, 1), :]
         th_row = thresh_ref[pl.ds(l, 1), :]
-
-        def mm(u, first, pairs):
-            rs = pl.ds(u * half, half)
-            for i, (dz, dy) in enumerate(pairs):
-                b = wrap(zc + dz) * SIDE + wrap(yc + dy)
-                rows = pl.ds(pl.multiple_of(b * feat, feat), feat)
-                val = jnp.dot(agbuf[b, rs], w_in_v[rows, :], preferred_element_type=F32)
-                if first and i == 0:
-                    proj[rs, :] = val
-                else:
-                    proj[rs, :] += val
-
-        near = ((0, 0), (0, 1), (0, -1), (1, 0), (-1, 0), (1, 1), (1, -1), (-1, 1), (-1, -1))
-        away = ((2, 0), (2, 1), (2, 2), (2, 3), (0, 2), (1, 2), (3, 2))
 
         def scan(u):
             for cb in range(ncb):
@@ -509,11 +513,8 @@
                     ein[s, :, cs] = jnp.where(sub >= 1, pltpu.roll(e, 1, 0), 0.0)
                     pin[s, :, cs] = jnp.where(sub >= 1, pltpu.roll(p, 1, 0), 1.0)
 
-        ag_wait(0, 6, 7, 10, 11, 14, 15, 18, 19)
-        mm(0, True, near + away)
         proj[:half, :] = proj[:half, :] * fac[:half]
         scan(0)
-        mm(1, True, near)
         ag_wait(1, 6, 7, 10, 11, 14, 15, 18, 19)
         mm(1, False, away)
         proj[half:, :] = proj[half:, :] * fac[half:]
@@ -588,23 +589,27 @@
         @pl.when(l + 1 < layers)
         def _():
             later_copies[2].wait()
-            regroup(0, nreg // 4)
+            regroup(0, nreg // 8)
 
         rs2(1)
         rs3(0)
 
         @pl.when(l + 1 < layers)
         def _():
-            regroup(nreg // 4, nreg // 2)
+            regroup(nreg // 8, nreg // 2)
 
         rs4(0)
 
         @pl.when(l + 1 < layers)
         def _():
             publish(l + 1, 0)
+
+        rs3(1)
+
+        @pl.when(l + 1 < layers)
+        def _():
             regroup(nreg // 2, nreg)
 
-        rs3(1)
         rs4(1)
         for u in range(2):
             for h in range(2):

time: 112 us -> 107 us (0.955)
  Pallas kernels: 110 us -> 106 us
    pallas_call x1, Pallas kernels: 110 us -> 106 us  [per_device(): pl.pallas_call(functools.partial(kernel_body, dims), out_shape=jax.ShapeD...]
where the time goes in v6:
time: 107 us
  Pallas kernels  106 us (99%)
  local copies, waits for them, and re-layouts  1.57 us (1%)
    pallas_call x1, Pallas kernels, per_device(): pl.pallas_call(functools.partial(kernel_body, dims), out_shape=jax.ShapeD...  106 us

profile of v6, /device:TPU:6, one launch (start us, length us, event | category | flops | bytes accessed | tf_op | source)
XLA Modules:
  0.0 107.3 jit_solution(3992450051306635784)
XLA Ops:
  0.0 105.7 %shard_map.100 = bf16[256,256]{1,0:T(8,128)(2,1)} custom-call(bf16[256,256]{1,0:T(8,128)(2,1)} %tok_ref.1, f32[2,4096]{1,0:T(2,128)} %gain_ref.1, bf16[2,32768,128]{2,1,0:T(8,128)(2,1)} %bitcast.6, bf16[2,288,256]{2,1,0:T(8,128)(2,1)} %bitcast.7, bf16[2,256,512]{2,1,0:T(8,128)(2,1)} %w_dt_hbm.1, f32[2,16,512]{2,1,0:T(8,128)} %a_ref.1, f32[2,512]{1,0:T(2,128)} %bias_ref.1, ...), custom_call_target="tpu_custom_call" | custom-call | tf_op jit(solution)/shard_map/pallas_call | solution.py:645
  105.7 1.6 %copy.13 = bf16[256,256]{1,0:T(8,128)(2,1)} copy(bf16[256,256]{1,0:T(8,128)(2,1)} %shard_map.100) | data formatting | bytes 262144

commit v7 on v6

--- a/solution.py
+++ b/solution.py
@@ -193,9 +193,9 @@
         gain_row = gain_ref[pl.ds(l, 1), pl.ds(pl.multiple_of(tpi * feat, feat), feat)]
         agbuf[tpi, rows] = (own * gain_row).astype(BF16)
         sqv[rows, :] = jnp.broadcast_to(jnp.sum(own * own, axis=1, keepdims=True), (half, LANE))
-        ag_start(u, 0, 1, 4, 5, 2)
 
     publish(0, 0)
+    ag_start(0, 0, 1, 4, 5, 2)
 
     ei = lax.broadcasted_iota(jnp.int32, (LANE, states * LANE), 0)
     ej = lax.broadcasted_iota(jnp.int32, (LANE, states * LANE), 1) // LANE
@@ -353,6 +353,7 @@
 
         for d in range(1, n_tp):
             ar1(d, True).start()
+        ag_start(1, 0, 1, 4, 5, 2)
 
         ag_wait(0, 0, 1)
         ag_start(0, 8, 9, 12, 13)
@@ -367,19 +368,6 @@
             for c in (first_copies[1], first_copies[3], later_copies[0], later_copies[1], later_copies[3]):
                 c.start()
             regroup(0, nreg // 4)
-
-        ag_wait(1, 0, 1)
-        ag_start(1, 8, 9, 12, 13)
-        ag_wait(1, 4, 5)
-        ag_start(1, 6, 7)
-        ag_wait(1, 2)
-        ag_start(1, 16, 17)
-        ag_wait(0, 8, 9)
-        ag_start(0, 10, 11)
-        ag_wait(0, 12, 13)
-        ag_start(0, 14, 15)
-        ag_wait(0, 16, 17)
-        ag_start(0, 18, 19)
 
         for d in range(1, n_tp):
             ar1(d, False).wait_recv()
@@ -404,6 +392,19 @@
 
         for d in range(1, n_tp):
             ar2(d, True).start()
+
+        ag_wait(0, 8, 9)
+        ag_start(0, 10, 11)
+        ag_wait(0, 12, 13)
+        ag_start(0, 14, 15)
+        ag_wait(0, 16, 17)
+        ag_start(0, 18, 19)
+        ag_wait(1, 0, 1)
+        ag_start(1, 8, 9, 12, 13)
+        ag_wait(1, 4, 5)
+        ag_start(1, 6, 7)
+        ag_wait(1, 2)
+        ag_start(1, 16, 17)
 
         @pl.when(l == 0)
         def _():
@@ -603,6 +604,7 @@
         @pl.when(l + 1 < layers)
         def _():
             publish(l + 1, 0)
+            ag_start(0, 0, 1, 4, 5, 2)
 
         rs3(1)
 

time: 107 us -> 113 us (1.056)
  Pallas kernels: 106 us -> 111 us
    pallas_call x1, Pallas kernels: 106 us -> 111 us  [per_device(): pl.pallas_call(functools.partial(kernel_body, dims), out_shape=jax.ShapeD...]
where the time goes in v7:
time: 113 us
  Pallas kernels  111 us (98%)
  local copies, waits for them, and re-layouts  1.57 us (1%)
    pallas_call x1, Pallas kernels, per_device(): pl.pallas_call(functools.partial(kernel_body, dims), out_shape=jax.ShapeD...  111 us

profile of v7, /device:TPU:6, one launch (start us, length us, event | category | flops | bytes accessed | tf_op | source)
XLA Modules:
  0.0 113.0 jit_solution(14876980470688928339)
XLA Ops:
  0.0 111.5 %shard_map.100 = bf16[256,256]{1,0:T(8,128)(2,1)} custom-call(bf16[256,256]{1,0:T(8,128)(2,1)} %tok_ref.1, f32[2,4096]{1,0:T(2,128)} %gain_ref.1, bf16[2,32768,128]{2,1,0:T(8,128)(2,1)} %bitcast.6, bf16[2,288,256]{2,1,0:T(8,128)(2,1)} %bitcast.7, bf16[2,256,512]{2,1,0:T(8,128)(2,1)} %w_dt_hbm.1, f32[2,16,512]{2,1,0:T(8,128)} %a_ref.1, f32[2,512]{1,0:T(2,128)} %bias_ref.1, ...), custom_call_target="tpu_custom_call" | custom-call | tf_op jit(solution)/shard_map/pallas_call | solution.py:647
  111.5 1.6 %copy.13 = bf16[256,256]{1,0:T(8,128)(2,1)} copy(bf16[256,256]{1,0:T(8,128)(2,1)} %shard_map.100) | data formatting | bytes 262144
